TPU v7x, 32 devices: a whole 2x2x4 slice. The times are simulated.
32 devices in a mesh: pts: 4 (over y, core), ctr: 8 (over z, x).
Axes of the slice: x: 2, y: 2, z: 4, core: 2. Of those that a mesh axis runs over, the one named last changes fastest.
Arguments:
- points: bfloat16 [512, 512], P(('pts', 'ctr')), may hold values from -6 to 6
- point_class: int32 [512], P(('pts', 'ctr')), may hold values from 0 to 7
- targets: float32 [512, 128], P(('pts', 'ctr')), may hold values from -6 to 6
- class_weight: float32 [8], replicated, may hold values from 0.25 to 4
- inv_scale: float32 [512], replicated, may hold values from 0.003 to 0.3
- centers: bfloat16 [32768, 512], P('ctr'), may hold values from -6 to 6
- coefficients: bfloat16 [32768, 128], P('ctr'), may hold values from -2.5 to 2.5
- center_index: int32 [4096], replicated, may hold values from 0 to 32767, as said below
- factor: float32 [4096, 4096], P('ctr'), as said below
- panel_inverse: float32 [4096, 2048], P('ctr'), as said below
Outputs:
- gradient: float32 [32768, 128], P('ctr', 'pts')
- solved: float32 [4096, 128], P('ctr', 'pts')
Inputs may be any that keep to these rules, and one draw needn't show every extreme that they name: `center_index`: the values are distinct; window row r lies in the center shard (index of ctr, 4096 centers each) numbered order[r mod 8] for one permutation order of the shards, so each shard holds exactly 512 window rows and the 512 rows of each aligned block of the window hold at most 64 of one shard's centers, a bound that is reached. factor is lower triangular with its diagonal between 1 and 2. `panel_inverse`: the rows of panel p hold the inverse of factor's diagonal block of rows and columns p * 2048 to (p + 1) * 2048 - 1.
All inputs are finite; a program needn't handle non-finite values.
Results may differ from a plain program's by a relative error of at most 0.0055.
Values may be sent and summed in bfloat16 or wider, within the bound.
A program may use at most 64 MiB of HBM per device.

v0:
```python
import functools

import jax
import jax.numpy as jnp
from jax import lax
from jax.experimental import pallas as pl
from jax.experimental.pallas import tpu as pltpu
from jax.sharding import PartitionSpec as P

MESH = pl.DeviceIdType.MESH
NT = (((1,), (1,)), ((), ()))
F32 = jnp.float32
BF16 = jnp.bfloat16


def dot_nt(left, right):
    return lax.dot_general(left, right, NT, preferred_element_type=F32)


def kernel(
    n_pts, n_ctr, panels, chunk,
    pts_ref, cls_ref, tgt_ref, cw_ref, inv_ref, idx_ref, idx_hbm, cen_hbm, coef_hbm, fac_hbm, pinv_hbm,
    grad_ref, sol_ref,
    cen, coef, pinv_raw, pinv, fac_raw, fac, rnorm, pall, kmat, ksel,
    head, sel, part, part_recv, rall, wsend, wrecv, wpack, wblk, solsend, solrecv, rhssend, rhsrecv,
    loc, pt_s, pt_r, fw_s, fw_r, pr_s, pr_r, rs_s, rs_r, w_s, w_r, so_s, so_r, rh_s, rh_r,
):
    p_me, c_me = lax.axis_index("pts"), lax.axis_index("ctr")
    rows = pts_ref.shape[0]
    group = rows * n_ctr
    centers = cen.shape[0]
    feats = cen.shape[1]
    targets = tgt_ref.shape[1]
    tcols = targets // n_pts
    own_rows = pinv.shape[0]
    panel_rows = pinv.shape[1]
    owners = panel_rows // own_rows
    my_panel = c_me // owners
    chunks = centers // chunk

    def remote(src, dst, send, recv, p, c):
        return pltpu.make_async_remote_copy(
            src_ref=src, dst_ref=dst, send_sem=send, recv_sem=recv,
            device_id={"pts": p, "ctr": c}, device_id_type=MESH,
        )

    def each(n, fn):
        def step(k, carry):
            fn(k)
            return carry
        lax.fori_loop(0, n, step, 0)

    barrier = pltpu.get_barrier_semaphore()
    everyone = n_pts * n_ctr
    me = p_me * n_ctr + c_me

    def greet(k):
        other = lax.rem(me + k + 1, everyone)
        pl.semaphore_signal(
            barrier, inc=1,
            device_id={"pts": other // n_ctr, "ctr": lax.rem(other, n_ctr)}, device_id_type=MESH,
        )
    cen_copy = pltpu.make_async_copy(cen_hbm, cen, loc.at[0])
    coef_copy = pltpu.make_async_copy(coef_hbm, coef, loc.at[1])
    pinv_copy = pltpu.make_async_copy(pinv_hbm, pinv_raw, loc.at[2])
    fac_copy = pltpu.make_async_copy(fac_hbm.at[:, pl.ds(0, fac.shape[1])], fac_raw, loc.at[3])
    head_copy = pltpu.make_async_copy(idx_hbm.at[pl.ds(0, head.shape[0])], head, loc.at[4])
    cen_copy.start()
    each(everyone - 1, greet)
    coef_copy.start()

    inv = inv_ref[...]
    own_slot = pl.ds(pl.multiple_of(me * rows, rows), rows)
    pall[own_slot, :] = (pts_ref[...].astype(F32) * inv).astype(BF16)
    pl.semaphore_wait(barrier, everyone - 1)

    def pt_copy(c_src, c_dst):
        slot = pl.ds(pl.multiple_of((p_me * n_ctr + c_src) * rows, rows), rows)
        return remote(pall.at[slot], pall.at[slot], pt_s.at[c_dst], pt_r.at[c_src], p_me, c_dst)

    def peer(k):
        return lax.rem(c_me + k + 1, n_ctr)
    each(n_ctr - 1, lambda k: pt_copy(c_me, peer(k)).start())

    ones = jnp.ones((8, feats), BF16)
    cen_copy.wait()

    def scale(k):
        at = pl.ds(pl.multiple_of(k * chunk, chunk), chunk)
        scaled = (cen[at, :].astype(F32) * inv).astype(BF16)
        cen[at, :] = scaled
        square = jnp.square(scaled.astype(F32))
        high = square.astype(BF16)
        low = (square - high.astype(F32)).astype(BF16)
        rnorm[:, at] = 0.5 * (dot_nt(ones, high) + dot_nt(ones, low))
    each(chunks, scale)
    coef_copy.wait()
    pinv_copy.start()
    fac_copy.start()
    head_copy.start()

    each(n_ctr - 1, lambda k: pt_copy(peer(k), peer(k)).wait_recv())

    def group_at(p):
        return pl.ds(pl.multiple_of(p * group, group), group)

    def fw_copy(p_src, p_dst):
        at = group_at(p_src)
        return remote(pall.at[at], pall.at[at], fw_s.at[p_dst], fw_r.at[p_src], p_dst, c_me)

    pair = p_me // 2 * 2

    def mate(k):
        return 2 * pair + 1 - p_me if k == 0 else lax.rem(pair + k + 1, n_pts)
    for k in range(n_pts - 1):
        fw_copy(p_me, mate(k)).start()

    def half_norm(x):
        return 0.5 * jnp.sum(jnp.square(x.astype(F32)), axis=1, keepdims=True)

    def kernel_block(p, k):
        at = pl.ds(pl.multiple_of(k * chunk, chunk), chunk)
        mine = pall[group_at(p), :]
        exponent = dot_nt(mine, cen[at, :]) - half_norm(mine) - rnorm[0:1, at]
        block = jnp.exp(exponent).astype(BF16)
        kmat[group_at(p), at] = block
        return block, at

    def forward(k, total):
        block, at = kernel_block(p_me, k)
        return total + jnp.dot(block, coef[at, :], preferred_element_type=F32)
    total = lax.fori_loop(0, chunks, forward, jnp.zeros((group, targets), F32))
    part[...] = total.reshape(n_ctr, rows, targets)

    def pr_copy(c_src, c_dst):
        return remote(part.at[c_dst], part_recv.at[c_src], pr_s.at[c_dst], pr_r.at[c_src], p_me, c_dst)
    each(n_ctr - 1, lambda k: pr_copy(c_me, peer(k)).start())

    shift, wide_lanes = 64, idx_ref.shape[1]
    per = wide_lanes // n_ctr
    slots = sel.shape[0]
    relative = idx_ref[...] - c_me * centers
    relative = jnp.where((relative >= 0) & (relative < centers), relative, 0)

    def iota(shape, dim):
        return lax.broadcasted_iota(jnp.int32, shape, dim)

    def hot(mask):
        return jnp.where(mask, 1.0, 0.0).astype(BF16)
    fold = hot(iota((wide_lanes, wide_lanes), 0) // n_ctr == iota((wide_lanes, wide_lanes), 1))
    spread = hot(iota((slots, relative.shape[0]), 0) // per == iota((slots, relative.shape[0]), 1))

    def column(value):
        folded = jnp.dot(value.astype(F32).astype(BF16), fold, preferred_element_type=F32)
        return jnp.dot(spread, folded.astype(BF16), preferred_element_type=F32)
    both = shift * column(relative // shift) + column(lax.rem(relative, shift))
    at_lane = lax.rem(iota((slots, wide_lanes), 0), per) == iota((slots, wide_lanes), 1)
    local_row = jnp.sum(jnp.where(at_lane, both, 0.0), axis=1, keepdims=True).astype(jnp.int32)
    sel[...] = jnp.zeros_like(sel)

    def select(k):
        at = pl.ds(pl.multiple_of(k * chunk, chunk), chunk)
        picked = hot(iota((slots, chunk), 1) == local_row - k * chunk)
        sel[...] += jnp.dot(picked, cen[at, :], preferred_element_type=F32)
    each(chunks, select)

    each(n_ctr - 1, lambda k: pr_copy(peer(k), peer(k)).wait_recv())
    part_recv[c_me] = part[c_me]
    predicted = jnp.sum(part_recv[...], axis=0)
    same = iota((rows, rows), 0) == iota((rows, rows), 1)
    own_class = jnp.sum(jnp.where(same, cls_ref[...], 0), axis=1, keepdims=True)
    classes = lax.broadcasted_iota(jnp.int32, (rows, cw_ref.shape[1]), 1)
    weight = jnp.sum(jnp.where(own_class == classes, cw_ref[...], 0.0), axis=1, keepdims=True)
    rall[own_slot, :] = (weight * (predicted - tgt_ref[...])).astype(BF16)

    def rs_copy(src, dst):
        slot = pl.ds(pl.multiple_of(src * rows, rows), rows)
        return remote(
            rall.at[slot], rall.at[slot], rs_s.at[dst], rs_r.at[src], dst // n_ctr, lax.rem(dst, n_ctr)
        )

    def other(k):
        return lax.rem(me + k + 1, everyone)
    each(everyone - 1, lambda k: rs_copy(me, other(k)).start())

    for k in range(n_pts - 1):
        fw_copy(mate(k), mate(k)).wait_recv()
        each(chunks, functools.partial(kernel_block, mate(k)))

    chosen = sel[...].astype(BF16)
    chosen_norm = half_norm(chosen)

    def window_kernel(p):
        mine = pall[group_at(p), :]
        square = jnp.square(mine.astype(F32))
        high = square.astype(BF16)
        low = (square - high.astype(F32)).astype(BF16)
        norm = 0.5 * (dot_nt(ones, high) + dot_nt(ones, low))
        ksel[:, group_at(p)] = jnp.exp(dot_nt(chosen, mine) - norm[0:1] - chosen_norm).astype(BF16)
    each(n_pts, window_kernel)

    each(everyone - 1, lambda k: rs_copy(other(k), other(k)).wait_recv())

    source = lax.broadcasted_iota(jnp.int32, (targets, targets), 0)
    lane = lax.broadcasted_iota(jnp.int32, (targets, targets), 1)
    pick = (source == p_me * tcols + lax.rem(lane, tcols)).astype(BF16)
    wide = jnp.dot(rall[...], pick, preferred_element_type=F32).astype(BF16)
    window = jnp.dot(ksel[...], wide, preferred_element_type=F32)
    run = wsend.shape[1]
    lane_group = lax.broadcasted_iota(jnp.int32, (run, targets), 1) // tcols
    for panel in range(panels):
        packed = jnp.zeros((run, targets), F32)
        for g in range(n_pts):
            begin = (panel * n_pts + g) * run
            packed = packed + jnp.where(lane_group == g, window[begin:begin + run], 0.0)
        wsend[panel] = packed.astype(BF16)

    def w_copy(c_src, c_dst):
        return remote(
            wsend.at[c_dst // owners], wrecv.at[c_src], w_s.at[c_dst], w_r.at[c_src], p_me, c_dst
        )
    each(n_ctr - 1, lambda k: w_copy(c_me, peer(k)).start())
    wrecv[c_me] = wsend[my_panel]

    tall = lax.broadcasted_iota(jnp.int32, (tcols, targets), 1)
    first = lax.broadcasted_iota(jnp.int32, (tcols, targets), 0)
    pick_t = (tall == p_me * tcols + first).astype(BF16)
    wide_t = dot_nt(pick_t, rall[...]).astype(BF16)

    def backward(k):
        at = pl.ds(pl.multiple_of(k * chunk, chunk), chunk)
        grad_ref[:, at] = jnp.dot(wide_t, kmat[:, at], preferred_element_type=F32)
    each(chunks, backward)
    pinv_copy.wait()
    fac_copy.wait()
    head_copy.wait()
    pinv[...] = pinv_raw[...].astype(BF16)

    each(n_ctr - 1, lambda k: w_copy(peer(k), peer(k)).wait_recv())
    for o in range(n_ctr):
        wpack[pl.ds(o, run, stride=n_ctr), :] = wrecv[head[o // wide_lanes, o % wide_lanes] // centers].astype(F32)

    def so_copy(c_src, c_dst):
        return remote(solsend, solrecv.at[c_src], so_s.at[c_dst], so_r.at[c_src], p_me, c_dst)

    def rh_copy(c_src, c_dst):
        at = lax.rem(c_src, owners)
        return remote(rhssend, rhsrecv.at[at], rh_s.at[c_dst], rh_r.at[at], p_me, c_dst)

    for panel in range(panels):
        @pl.when(my_panel == panel)
        def _():
            if panel == 0:
                turned = wpack[...].T.astype(BF16)
                rhs = jnp.concatenate([turned[g * tcols:(g + 1) * tcols] for g in range(n_pts)], axis=1)
            else:
                local = (c_me - panel * owners) * own_rows
                part_len = panel_rows // n_pts
                within = pl.multiple_of(lax.rem(local, part_len), own_rows)
                turned = wpack[pl.ds(within, own_rows), :].T
                for g in range(n_pts):
                    wblk[g] = turned[g * tcols:(g + 1) * tcols]
                own = wblk[local // part_len]
                done = panel * owners
                fac[...] = fac_raw[...].astype(BF16)
                each(done, lambda k: so_copy(k, k).wait_recv())
                solved = jnp.concatenate([solrecv[b] for b in range(done)], axis=1)
                own = own - dot_nt(solved, fac[:, :done * own_rows])
                rhssend[...] = own.astype(BF16)

                def fellow(k):
                    return panel * owners + lax.rem(c_me - panel * owners + k + 1, owners)
                each(owners - 1, lambda k: rh_copy(c_me, fellow(k)).start())
                rhsrecv[c_me - panel * owners] = rhssend[...]
                each(owners - 1, lambda k: rh_copy(fellow(k), fellow(k)).wait_recv())
                rhs = jnp.concatenate([rhsrecv[b] for b in range(owners)], axis=1)
            result = dot_nt(rhs, pinv[...])
            sol_ref[...] = result
            later = (panels - 1 - panel) * owners
            if later:
                solsend[...] = result.astype(BF16)

                def after(k):
                    return (panel + 1) * owners + lax.rem(k + c_me, later)
                each(later, lambda k: so_copy(c_me, after(k)).start())
                each(later, lambda k: so_copy(c_me, after(k)).wait_send())
            if panel > 0:
                each(owners - 1, lambda k: rh_copy(c_me, fellow(k)).wait_send())

    each(n_ctr - 1, lambda k: pt_copy(c_me, peer(k)).wait_send())
    for k in range(n_pts - 1):
        fw_copy(p_me, mate(k)).wait_send()
    each(n_ctr - 1, lambda k: pr_copy(c_me, peer(k)).wait_send())
    each(everyone - 1, lambda k: rs_copy(me, other(k)).wait_send())
    each(n_ctr - 1, lambda k: w_copy(c_me, peer(k)).wait_send())


def body(
    points, point_class, targets, class_weight, inv_scale, centers, coefficients, center_index, factor, panel_inverse
):
    n_pts, n_ctr = lax.axis_size("pts"), lax.axis_size("ctr")
    rows, feats = points.shape
    n_cen, n_tgt = coefficients.shape
    tcols = n_tgt // n_pts
    own_rows, panel_rows = panel_inverse.shape
    panels = factor.shape[1] // panel_rows
    owners = panel_rows // own_rows
    everyone = n_pts * n_ctr
    total = rows * everyone
    slots = center_index.shape[0] // n_ctr
    run = slots // panels // n_pts
    solved_cols = panel_rows * (panels - 1)
    index = center_index.reshape(-1, 128)
    vmem = pl.BlockSpec(memory_space=pltpu.VMEM)
    hbm = pl.BlockSpec(memory_space=pl.ANY)
    dma = pltpu.SemaphoreType.DMA
    scratch = [
        pltpu.VMEM((n_cen, feats), BF16),
        pltpu.VMEM((n_cen, n_tgt), BF16),
        pltpu.VMEM((own_rows, panel_rows), F32),
        pltpu.VMEM((own_rows, panel_rows), BF16),
        pltpu.VMEM((own_rows, solved_cols), F32),
        pltpu.VMEM((own_rows, solved_cols), BF16),
        pltpu.VMEM((8, n_cen), F32),
        pltpu.VMEM((total, feats), BF16),
        pltpu.VMEM((total, n_cen), BF16),
        pltpu.VMEM((slots, total), BF16),
        pltpu.SMEM((8, 128), jnp.int32),
        pltpu.VMEM((slots, feats), F32),
        pltpu.VMEM((n_ctr, rows, n_tgt), F32),
        pltpu.VMEM((n_ctr, rows, n_tgt), F32),
        pltpu.VMEM((total, n_tgt), BF16),
        pltpu.VMEM((panels, run, n_tgt), BF16),
        pltpu.VMEM((n_ctr, run, n_tgt), BF16),
        pltpu.VMEM((run * n_ctr, n_tgt), F32),
        pltpu.VMEM((n_pts, tcols, own_rows), F32),
        pltpu.VMEM((tcols, own_rows), BF16),
        pltpu.VMEM((owners * (panels - 1), tcols, own_rows), BF16),
        pltpu.VMEM((tcols, own_rows), BF16),
        pltpu.VMEM((owners, tcols, own_rows), BF16),
        dma((5,)),
        dma((n_ctr,)), dma((n_ctr,)),
        dma((n_pts,)), dma((n_pts,)),
        dma((n_ctr,)), dma((n_ctr,)),
        dma((everyone,)), dma((everyone,)),
        dma((n_ctr,)), dma((n_ctr,)),
        dma((n_ctr,)), dma((n_ctr,)),
        dma((n_ctr,)), dma((owners,)),
    ]
    grad, solved = pl.pallas_call(
        functools.partial(kernel, n_pts, n_ctr, panels, 1024),
        out_shape=(
            jax.ShapeDtypeStruct((tcols, n_cen), F32),
            jax.ShapeDtypeStruct((tcols, own_rows), F32),
        ),
        in_specs=[vmem] * 6 + [hbm] * 5,
        out_specs=(vmem, vmem),
        scratch_shapes=scratch,
        compiler_params=pltpu.CompilerParams(
            collective_id=0, has_side_effects=True, vmem_limit_bytes=67043328
        ),
        name="falkon",
    )(
        points, point_class[None, :], targets, class_weight[None, :], inv_scale[None, :],
        index, index, centers, coefficients, factor, panel_inverse,
    )
    return grad.T, solved.T


def solution(mesh):
    placed = (
        P(("pts", "ctr"), None),
        P(("pts", "ctr")),
        P(("pts", "ctr"), None),
        P(),
        P(),
        P("ctr", None),
        P("ctr", None),
        P(),
        P("ctr", None),
        P("ctr", None),
    )
    return jax.shard_map(
        body,
        mesh=mesh,
        in_specs=placed,
        out_specs=(P("ctr", "pts"), P("ctr", "pts")),
        check_vma=False,
    )
```

profile of v0, /device:TPU:18, one launch (start us, length us, event | category | flops | bytes accessed | tf_op | source)
XLA Modules:
  0.0 48.8 jit_solution(11285277159207758075)
XLA Ops:
  0.6 44.8 %falkon.1 = (f32[32,4096]{1,0:T(8,128)}, f32[32,512]{1,0:T(8,128)}) custom-call(bf16[16,512]{1,0:T(8,128)(2,1)} %pts_ref.1, s32[1,16]{1,0:T(1,128)} %bitcast.11, f32[16,128]{1,0:T(8,128)} %tgt_ref.1, f32[1,8]{1,0:T(1,128)} %bitcast.12, f32[1,512]{1,0:T(1,128)} %bitcast.10, s32[32,128]{1,0:T(8,128)} %bitcast.7, s32[32,128]{1,0:T(8,128)} %bitcast.8, ...), custom_call_target="tpu_custom_call" | custom-call | tf_op jit(solution)/shard_map/falkon/pallas_call | solution.py:350
  45.5 1.9 %copy.14 = f32[4096,32]{0,1:T(8,128)} copy(f32[4096,32]{0,1:T(8,128)} %bitcast.6) | data formatting | bytes 1048576
  47.3 1.5 %copy.15 = f32[512,32]{0,1:T(8,128)} copy(f32[512,32]{0,1:T(8,128)} %bitcast.9) | data formatting | bytes 131072
where the time goes:
time: 49.1 us; the launch traced here: 48.8 us
  Pallas kernels  44.8 us (91%)
  local copies, waits for them, and re-layouts  3.34 us (7%)
  between operations  0.64 us (1%)
    pallas_call x1, Pallas kernels, body(): pl.pallas_call(functools.partial(kernel, n_pts, n_ctr, panels, 1024), out...  44.8 us
    unnamed x2, local copies, waits for them, and re-layouts  3.34 us

commit v1 on v0

--- a/solution.py
+++ b/solution.py
@@ -295,6 +295,15 @@
     each(n_ctr - 1, lambda k: w_copy(c_me, peer(k)).wait_send())
 
 
+def emit(grad_ref, sol_ref, grad_out, sol_out, sem):
+    first = pltpu.make_async_copy(grad_ref, grad_out, sem.at[0])
+    second = pltpu.make_async_copy(sol_ref, sol_out, sem.at[1])
+    first.start()
+    second.start()
+    first.wait()
+    second.wait()
+
+
 def body(
     points, point_class, targets, class_weight, inv_scale, centers, coefficients, center_index, factor, panel_inverse
 ):
@@ -312,7 +321,7 @@
     solved_cols = panel_rows * (panels - 1)
     index = center_index.reshape(-1, 128)
     vmem = pl.BlockSpec(memory_space=pltpu.VMEM)
-    hbm = pl.BlockSpec(memory_space=pl.ANY)
+    hbm = pl.BlockSpec(memory_space=pltpu.HBM)
     dma = pltpu.SemaphoreType.DMA
     scratch = [
         pltpu.VMEM((n_cen, feats), BF16),
@@ -350,20 +359,32 @@
     grad, solved = pl.pallas_call(
         functools.partial(kernel, n_pts, n_ctr, panels, 1024),
         out_shape=(
-            jax.ShapeDtypeStruct((tcols, n_cen), F32),
-            jax.ShapeDtypeStruct((tcols, own_rows), F32),
+            pltpu.VMEM((tcols, n_cen), F32),
+            pltpu.VMEM((tcols, own_rows), F32),
         ),
         in_specs=[vmem] * 6 + [hbm] * 5,
         out_specs=(vmem, vmem),
         scratch_shapes=scratch,
         compiler_params=pltpu.CompilerParams(
-            collective_id=0, has_side_effects=True, vmem_limit_bytes=67043328
+            collective_id=0, has_side_effects=True, vmem_limit_bytes=60000000
         ),
         name="falkon",
     )(
         points, point_class[None, :], targets, class_weight[None, :], inv_scale[None, :],
         index, index, centers, coefficients, factor, panel_inverse,
     )
+    grad, solved = pl.pallas_call(
+        emit,
+        out_shape=(
+            jax.ShapeDtypeStruct((tcols, n_cen), F32),
+            jax.ShapeDtypeStruct((tcols, own_rows), F32),
+        ),
+        in_specs=[vmem, vmem],
+        out_specs=(hbm, hbm),
+        scratch_shapes=[dma((2,))],
+        compiler_params=pltpu.CompilerParams(vmem_limit_bytes=1048576),
+        name="emit",
+    )(grad, solved)
     return grad.T, solved.T
 
 

time: 49.1 us -> 45.7 us (0.931)
  local copies, waits for them, and re-layouts: 3.34 us -> 0 us
    unnamed x2 -> x0, local copies, waits for them, and re-layouts: 3.34 us -> none
    pallas_call x1, Pallas kernels: 44.8 us -> 44 us  [body(): pl.pallas_call(functools.partial(kernel, n_pts, n_ctr, panels, 1024), out...]
    pallas_call x0 -> x1, Pallas kernels: none -> 0.82 us  [body(): pl.pallas_call(emit, out_shape=(jax.ShapeDtypeStruct((tcols, n_cen), F32)...]
where the time goes in v1:
time: 45.7 us; the launch traced here: 45.4 us
  Pallas kernels  44.8 us (98%)
  between operations  0.64 us (1%)
    pallas_call x1, Pallas kernels, body(): pl.pallas_call(functools.partial(kernel, n_pts, n_ctr, panels, 1024), out...  44 us

profile of v1, /device:TPU:18, one launch (start us, length us, event | category | flops | bytes accessed | tf_op | source)
XLA Modules:
  0.0 45.4 jit_solution(2456016214208049417)
XLA Ops:
  0.6 44.0 %falkon.1 = (f32[32,4096]{1,0:T(8,128)S(1)}, f32[32,512]{1,0:T(8,128)S(1)}) custom-call(bf16[16,512]{1,0:T(8,128)(2,1)} %pts_ref.1, s32[1,16]{1,0:T(1,128)} %bitcast.9, f32[16,128]{1,0:T(8,128)} %tgt_ref.1, f32[1,8]{1,0:T(1,128)} %bitcast.10, f32[1,512]{1,0:T(1,128)} %bitcast.8, s32[32,128]{1,0:T(8,128)} %bitcast.6, s32[32,128]{1,0:T(8,128)} %bitcast.7, ...), custom_call_target="tpu_custom_call" | custom-call | tf_op jit(solution)/shard_map/falkon/pallas_call | solution.py:359
  44.6 0.8 %emit.1 = (f32[32,4096]{1,0:T(8,128)}, f32[32,512]{1,0:T(8,128)}) custom-call(f32[32,4096]{1,0:T(8,128)S(1)} %get-tuple-element.6.grad_ref, f32[32,512]{1,0:T(8,128)S(1)} %get-tuple-element.7.sol_ref), custom_call_target="tpu_custom_call" | custom-call | tf_op jit(solution)/shard_map/emit/pallas_call | solution.py:376

commit v2 on v1

v2 whole, which is shorter than its diff:
```python
import functools

import jax
import jax.numpy as jnp
from jax import lax
from jax.experimental import pallas as pl
from jax.experimental.pallas import tpu as pltpu
from jax.sharding import PartitionSpec as P

MESH = pl.DeviceIdType.MESH
NT = (((1,), (1,)), ((), ()))
F32 = jnp.float32
BF16 = jnp.bfloat16
LANES = 128


def dot_nt(left, right):
    return lax.dot_general(left, right, NT, preferred_element_type=F32)


def iota(shape, dim):
    return lax.broadcasted_iota(jnp.int32, shape, dim)


def hot(mask):
    return jnp.where(mask, 1.0, 0.0).astype(BF16)


def half_norm(x):
    return 0.5 * jnp.sum(jnp.square(x.astype(F32)), axis=1, keepdims=True)


def half_norm_row(x):
    square = jnp.square(x.astype(F32))
    folded = square[:, :LANES]
    for begin in range(LANES, square.shape[1], LANES):
        folded = folded + square[:, begin:begin + LANES]
    return 0.5 * jnp.sum(folded.T, axis=0, keepdims=True)


def each(n, fn):
    def step(k, carry):
        fn(k)
        return carry
    lax.fori_loop(0, n, step, 0)


def kernel(
    n_pts, n_ctr, panels, chunk, sub,
    pts_hbm, cls_hbm, tgt_hbm, cw_hbm, inv_hbm, idx_hbm, cen_hbm, coef_hbm, fac_hbm, pinv_hbm,
    grad_ref, sol_ref,
    pts, cls, tgt, cw, inv_row, idx, head,
    cen, coef, pinv_raw, pinv, fac_raw, fac, rnorm, pnorm, pall, kmat, ksel,
    sel, total_acc, part, part_recv, wt_send, wt_recv, rsend, rbuf,
    wsend, wrecv, wpack, wblk, solsend, solrecv, rhssend, rhsrecv,
    loc, cen_sem, pt_s, pt_r, fw_s, fw_r, pr_s, pr_r, wt_s, wt_r, rs_s, rs_r, w_s, w_r, so_s, so_r, rh_s, rh_r,
):
    p_me, c_me = lax.axis_index("pts"), lax.axis_index("ctr")
    rows, feats = pts.shape
    group = rows * n_ctr
    centers = cen.shape[0]
    targets = tgt.shape[1]
    tcols = targets // n_pts
    own_rows, panel_rows = pinv.shape
    owners = panel_rows // own_rows
    my_panel = c_me // owners
    chunks = centers // chunk
    blocks = rbuf.shape[0]
    pt_blocks = blocks // n_pts
    per_block = n_ctr // pt_blocks
    copies = n_ctr // blocks
    width = rows * per_block
    me = p_me * n_ctr + c_me
    blk = lax.rem(c_me, blocks)
    rep = c_me // blocks
    blk_pts = lax.rem(blk, n_pts)
    own_block = blk_pts == p_me

    def remote(src, dst, send, recv, p, c):
        return pltpu.make_async_remote_copy(
            src_ref=src, dst_ref=dst, send_sem=send, recv_sem=recv,
            device_id={"pts": p, "ctr": c}, device_id_type=MESH,
        )

    def local(src, dst, k):
        return pltpu.make_async_copy(src, dst, loc.at[k])

    def cen_copy(k):
        at = pl.ds(pl.multiple_of(k * chunk, chunk), chunk)
        return pltpu.make_async_copy(cen_hbm.at[at], cen.at[at], cen_sem.at[k])

    pts_copy = local(pts_hbm, pts, 0)
    inv_copy = local(inv_hbm, inv_row, 1)
    cls_copy = local(cls_hbm, cls, 2)
    cw_copy = local(cw_hbm, cw, 3)
    tgt_copy = local(tgt_hbm, tgt, 4)
    idx_copy = local(idx_hbm, idx, 5)
    head_copy = local(idx_hbm.at[pl.ds(0, head.shape[0])], head, 6)
    coef_copy = local(coef_hbm, coef, 7)
    pinv_copy = local(pinv_hbm, pinv_raw, 8)
    fac_copy = local(fac_hbm.at[:, pl.ds(0, fac.shape[1])], fac_raw, 9)
    pts_copy.start()
    inv_copy.start()

    barrier = pltpu.get_barrier_semaphore()

    def peer(k):
        return lax.rem(c_me + k + 1, n_ctr)
    pair = p_me // 2 * 2

    def mate(k):
        return 2 * pair + 1 - p_me if k == 0 else lax.rem(pair + k + 1, n_pts)

    def source(k):
        p = lax.rem(p_me + k, n_pts)
        b = lax.rem(blk // n_pts + k // n_pts, pt_blocks)
        return p, b, rep * blocks + b * n_pts + p_me

    def greet(p, c):
        pl.semaphore_signal(barrier, inc=1, device_id={"pts": p, "ctr": c}, device_id_type=MESH)

    def foreign(k):
        return jnp.logical_or(k != 0, jnp.logical_not(own_block))

    each(n_ctr - 1, lambda k: greet(p_me, peer(k)))
    for k in range(n_pts - 1):
        greet(mate(k), c_me)

    def greet_source(k):
        @pl.when(foreign(k))
        def _():
            p, _, c = source(k)
            greet(p, c)
    each(blocks, greet_source)
    cls_copy.start()
    cw_copy.start()
    each(chunks, lambda k: cen_copy(k).start())
    idx_copy.start()
    tgt_copy.start()
    head_copy.start()
    coef_copy.start()

    pts_copy.wait()
    inv_copy.wait()
    inv = inv_row[...]
    own_slot = pl.ds(pl.multiple_of(me * rows, rows), rows)
    pall[own_slot, :] = (pts[...].astype(F32) * inv).astype(BF16)
    pl.semaphore_wait(barrier, n_ctr + n_pts - 2 + blocks - own_block.astype(jnp.int32))

    def pt_copy(c_src, c_dst):
        slot = pl.ds(pl.multiple_of((p_me * n_ctr + c_src) * rows, rows), rows)
        return remote(pall.at[slot], pall.at[slot], pt_s.at[c_dst], pt_r.at[c_src], p_me, c_dst)
    each(n_ctr - 1, lambda k: pt_copy(c_me, peer(k)).start())

    cls_copy.wait()
    cw_copy.wait()
    lane_of = lax.rem(c_me, per_block) * rows
    place = hot(iota((rows, width), 1) == iota((rows, width), 0) + lane_of)
    label = jnp.dot(
        jnp.broadcast_to(cls[...].astype(F32).astype(BF16), (8, rows)), place, preferred_element_type=F32
    )
    mine_lane = (iota((8, width), 1) >= lane_of) & (iota((8, width), 1) < lane_of + rows)
    weight = jnp.zeros((8, width), F32)
    for k in range(cw.shape[1]):
        weight = jnp.where(mine_lane & (label == float(k)), cw[0, k], weight)
    wt_send[...] = weight

    def wt_dest(k):
        turn = lax.rem(c_me + k, per_block)
        return turn // n_pts * blocks + c_me // per_block * n_pts + lax.rem(turn, n_pts)

    def wt_src(k):
        return blk // n_pts * per_block + k

    def wt_copy(c_src, c_dst):
        at = lax.rem(c_src, per_block)
        return remote(wt_send, wt_recv.at[at], wt_s.at[c_dst], wt_r.at[at], p_me, c_dst)

    def not_me(c, fn):
        @pl.when(c != c_me)
        def _():
            fn(c)
    each(per_block, lambda k: not_me(wt_dest(k), lambda c: wt_copy(c_me, c).start()))

    @pl.when(c_me // per_block == blk // n_pts)
    def _():
        wt_recv[lax.rem(c_me, per_block)] = weight

    step = 256

    def scale(k):
        at = pl.ds(pl.multiple_of(k * step, step), step)
        scaled = (cen[at, :].astype(F32) * inv).astype(BF16)
        cen[at, :] = scaled
        rnorm[0:1, at] = half_norm_row(scaled)

    def scale_chunk(k):
        cen_copy(k).wait()
        each(chunk // step, lambda j: scale(k * (chunk // step) + j))
    each(chunks, scale_chunk)

    idx_copy.wait()
    shift, wide_lanes = 64, idx.shape[1]
    per = wide_lanes // n_ctr
    slots = sel.shape[0]
    relative = idx[...] - c_me * centers
    relative = jnp.where((relative >= 0) & (relative < centers), relative, 0)
    fold = hot(iota((wide_lanes, wide_lanes), 0) // n_ctr == iota((wide_lanes, wide_lanes), 1))
    spread = hot(iota((slots, relative.shape[0]), 0) // per == iota((slots, relative.shape[0]), 1))

    def column(value):
        folded = jnp.dot(value.astype(F32).astype(BF16), fold, preferred_element_type=F32)
        return jnp.dot(spread, folded.astype(BF16), preferred_element_type=F32)
    both = shift * column(relative // shift) + column(lax.rem(relative, shift))
    at_lane = lax.rem(iota((slots, wide_lanes), 0), per) == iota((slots, wide_lanes), 1)
    local_row = jnp.sum(jnp.where(at_lane, both, 0.0), axis=1, keepdims=True).astype(jnp.int32)
    coef_copy.wait()
    tgt_copy.wait()
    head_copy.wait()
    pinv_copy.start()
    fac_copy.start()

    each(n_ctr - 1, lambda k: pt_copy(peer(k), peer(k)).wait_recv())

    def group_at(p):
        return pl.ds(pl.multiple_of(p * group, group), group)

    def fw_copy(p_src, p_dst):
        at = group_at(p_src)
        return remote(pall.at[at], pall.at[at], fw_s.at[p_dst], fw_r.at[p_src], p_dst, c_me)
    for k in range(n_pts - 1):
        fw_copy(p_me, mate(k)).start()

    def sub_at(k, j):
        return pl.ds(pl.multiple_of(k * chunk + j * sub, sub), sub)

    def kernel_block(left, norm, at):
        return jnp.exp(dot_nt(left, cen[at, :]) - norm - rnorm[0:1, at]).astype(BF16)
    mine = pall[group_at(p_me), :]
    mine_norm = half_norm(mine)
    pnorm[group_at(p_me), :] = jnp.broadcast_to(mine_norm, (group, LANES))

    def forward(k, total):
        at = pl.ds(pl.multiple_of(k * chunk, chunk), chunk)
        block = kernel_block(mine, mine_norm, at)
        kmat[group_at(p_me), at] = block
        return total + jnp.dot(block, coef[at, :], preferred_element_type=F32)
    total = jnp.zeros((group, targets), F32)
    for k in range(chunks):
        total = forward(k, total)
    total_acc[...] = total
    own_rows_at = pl.ds(pl.multiple_of(c_me * rows, rows), rows)
    total_acc[own_rows_at, :] = total_acc[own_rows_at, :] - tgt[...]
    for b in range(pt_blocks):
        turned = total_acc[b * width:(b + 1) * width, :].T
        for q in range(n_pts):
            part[b * n_pts + q] = turned[q * tcols:(q + 1) * tcols]

    def pr_copy(c_src, c_dst):
        return remote(
            part.at[lax.rem(c_dst, blocks)], part_recv.at[c_src], pr_s.at[c_dst], pr_r.at[c_src], p_me, c_dst
        )
    each(n_ctr - 1, lambda k: pr_copy(c_me, peer(k)).start())
    part_recv[c_me] = part[blk]

    sel[...] = jnp.zeros_like(sel)

    def select(k):
        at = pl.ds(pl.multiple_of(k * chunk, chunk), chunk)
        picked = hot(iota((slots, chunk), 1) == local_row - k * chunk)
        sel[...] += jnp.dot(picked, cen[at, :], preferred_element_type=F32)
    each(chunks, select)

    each(per_block, lambda k: not_me(wt_src(k), lambda c: wt_copy(c, c).wait_recv()))
    weights = jnp.sum(wt_recv[...], axis=0)[0:1]
    each(n_ctr - 1, lambda k: pr_copy(peer(k), peer(k)).wait_recv())
    residual = (weights * jnp.sum(part_recv[...], axis=0)).astype(BF16)
    rsend[...] = residual

    def rs_slot(p, b):
        return p * pt_blocks + b

    def rs_copy(p_src, b_src, p_dst, c_dst):
        at = rs_slot(p_src, b_src)
        return remote(rsend, rbuf.at[at], rs_s.at[lax.rem(c_dst, blocks)], rs_r.at[at], p_dst, c_dst)

    def rs_out(k):
        return rs_copy(p_me, blk // n_pts, blk_pts, rep * blocks + lax.rem(blk + k, blocks))

    def rs_in(k):
        p, b, _ = source(k)
        return rs_copy(p, b, p_me, c_me)

    def rs_each(fn):
        def step(k):
            @pl.when(foreign(k))
            def _():
                fn(k)
        each(blocks, step)
    rs_each(lambda k: rs_out(k).start())

    @pl.when(own_block)
    def _():
        rbuf[rs_slot(p_me, blk // n_pts)] = residual

    for k in range(n_pts - 1):
        fw_copy(mate(k), mate(k)).wait_recv()
    together = n_pts - 1 if group * n_pts <= 512 else 1
    for first in range(0, n_pts - 1, together):
        mates = [mate(k) for k in range(first, first + together)]
        left = jnp.concatenate([pall[group_at(p), :] for p in mates], axis=0)
        left_norm = half_norm(left)
        for k, p in enumerate(mates):
            pnorm[group_at(p), :] = jnp.broadcast_to(left_norm[k * group:(k + 1) * group], (group, LANES))

        def fill(k):
            for j in range(chunk // sub):
                at = sub_at(k, j)
                block = kernel_block(left, left_norm, at)
                for n, p in enumerate(mates):
                    kmat[group_at(p), at] = block[n * group:(n + 1) * group]
        each(chunks, fill)

    chosen = sel[...].astype(BF16)
    chosen_norm = half_norm(chosen)
    span = 512

    def window_kernel(k):
        at = pl.ds(pl.multiple_of(k * span, span), span)
        norm = pnorm[at, :].T[0:1]
        ksel[:, at] = jnp.exp(dot_nt(chosen, pall[at, :]) - norm - chosen_norm).astype(BF16)
    each(pall.shape[0] // span, window_kernel)

    rs_each(lambda k: rs_in(k).wait_recv())

    wide_t = jnp.concatenate([rbuf[b] for b in range(blocks)], axis=1)
    window = dot_nt(ksel[...], jnp.concatenate([wide_t] * n_pts, axis=0))
    run = wsend.shape[1]
    lane_group = iota((run, targets), 1) // tcols
    for panel in range(panels):
        packed = jnp.zeros((run, targets), F32)
        for g in range(n_pts):
            begin = (panel * n_pts + g) * run
            packed = packed + jnp.where(lane_group == g, window[begin:begin + run], 0.0)
        wsend[panel] = packed.astype(BF16)

    def w_copy(c_src, c_dst):
        return remote(
            wsend.at[c_dst // owners], wrecv.at[c_src], w_s.at[c_dst], w_r.at[c_src], p_me, c_dst
        )
    each(n_ctr - 1, lambda k: w_copy(c_me, peer(k)).start())
    wrecv[c_me] = wsend[my_panel]

    def backward(k):
        at = pl.ds(pl.multiple_of(k * chunk, chunk), chunk)
        grad_ref[:, at] = jnp.dot(wide_t, kmat[:, at], preferred_element_type=F32)
    each(chunks, backward)
    pinv_copy.wait()
    fac_copy.wait()
    pinv[...] = pinv_raw[...].astype(BF16)

    each(n_ctr - 1, lambda k: pt_copy(c_me, peer(k)).wait_send())
    each(per_block, lambda k: not_me(wt_dest(k), lambda c: wt_copy(c_me, c).wait_send()))
    for k in range(n_pts - 1):
        fw_copy(p_me, mate(k)).wait_send()
    each(n_ctr - 1, lambda k: pr_copy(c_me, peer(k)).wait_send())
    rs_each(lambda k: rs_out(k).wait_send())

    each(n_ctr - 1, lambda k: w_copy(peer(k), peer(k)).wait_recv())
    for o in range(n_ctr):
        wpack[pl.ds(o, run, stride=n_ctr), :] = wrecv[head[o // wide_lanes, o % wide_lanes] // centers].astype(F32)

    def so_copy(c_src, c_dst):
        return remote(solsend, solrecv.at[c_src], so_s.at[c_dst], so_r.at[c_src], p_me, c_dst)

    def rh_copy(c_src, c_dst):
        at = lax.rem(c_src, owners)
        return remote(rhssend, rhsrecv.at[at], rh_s.at[c_dst], rh_r.at[at], p_me, c_dst)

    for panel in range(panels):
        @pl.when(my_panel == panel)
        def _():
            if panel == 0:
                turned = wpack[...].T.astype(BF16)
                rhs = jnp.concatenate([turned[g * tcols:(g + 1) * tcols] for g in range(n_pts)], axis=1)
            else:
                offset = (c_me - panel * owners) * own_rows
                part_len = panel_rows // n_pts
                within = pl.multiple_of(lax.rem(offset, part_len), own_rows)
                turned = wpack[pl.ds(within, own_rows), :].T
                for g in range(n_pts):
                    wblk[g] = turned[g * tcols:(g + 1) * tcols]
                own = wblk[offset // part_len]
                done = panel * owners
                fac[...] = fac_raw[...].astype(BF16)
                each(done, lambda k: so_copy(k, k).wait_recv())
                solved = jnp.concatenate([solrecv[b] for b in range(done)], axis=1)
                own = own - dot_nt(solved, fac[:, :done * own_rows])
                rhssend[...] = own.astype(BF16)

                def fellow(k):
                    return panel * owners + lax.rem(c_me - panel * owners + k + 1, owners)
                each(owners - 1, lambda k: rh_copy(c_me, fellow(k)).start())
                rhsrecv[c_me - panel * owners] = rhssend[...]
                each(owners - 1, lambda k: rh_copy(fellow(k), fellow(k)).wait_recv())
                rhs = jnp.concatenate([rhsrecv[b] for b in range(owners)], axis=1)
            result = dot_nt(rhs, pinv[...])
            sol_ref[...] = result
            later = (panels - 1 - panel) * owners
            if later:
                solsend[...] = result.astype(BF16)

                def after(k):
                    return (panel + 1) * owners + lax.rem(k + c_me, later)
                each(later, lambda k: so_copy(c_me, after(k)).start())
                each(later, lambda k: so_copy(c_me, after(k)).wait_send())
            if panel > 0:
                each(owners - 1, lambda k: rh_copy(c_me, fellow(k)).wait_send())

    each(n_ctr - 1, lambda k: w_copy(c_me, peer(k)).wait_send())


def emit(grad_ref, sol_ref, grad_out, sol_out, sem):
    first = pltpu.make_async_copy(grad_ref, grad_out, sem.at[0])
    second = pltpu.make_async_copy(sol_ref, sol_out, sem.at[1])
    first.start()
    second.start()
    first.wait()
    second.wait()


def body(
    points, point_class, targets, class_weight, inv_scale, centers, coefficients, center_index, factor, panel_inverse
):
    n_pts, n_ctr = lax.axis_size("pts"), lax.axis_size("ctr")
    rows, feats = points.shape
    n_cen, n_tgt = coefficients.shape
    tcols = n_tgt // n_pts
    own_rows, panel_rows = panel_inverse.shape
    panels = factor.shape[1] // panel_rows
    owners = panel_rows // own_rows
    total = rows * n_pts * n_ctr
    group = rows * n_ctr
    per_block = LANES // rows
    pt_blocks = n_ctr // per_block
    blocks = n_pts * pt_blocks
    slots = center_index.shape[0] // n_ctr
    run = slots // panels // n_pts
    solved_cols = panel_rows * (panels - 1)
    chunk = 1024
    index = center_index.reshape(-1, LANES)
    vmem = pl.BlockSpec(memory_space=pltpu.VMEM)
    hbm = pl.BlockSpec(memory_space=pltpu.HBM)
    dma = pltpu.SemaphoreType.DMA
    scratch = [
        pltpu.VMEM((rows, feats), BF16),
        pltpu.VMEM((1, rows), jnp.int32),
        pltpu.VMEM((rows, n_tgt), F32),
        pltpu.SMEM((1, class_weight.shape[0]), F32),
        pltpu.VMEM((1, feats), F32),
        pltpu.VMEM(index.shape, jnp.int32),
        pltpu.SMEM((8, LANES), jnp.int32),
        pltpu.VMEM((n_cen, feats), BF16),
        pltpu.VMEM((n_cen, n_tgt), BF16),
        pltpu.VMEM((own_rows, panel_rows), F32),
        pltpu.VMEM((own_rows, panel_rows), BF16),
        pltpu.VMEM((own_rows, solved_cols), F32),
        pltpu.VMEM((own_rows, solved_cols), BF16),
        pltpu.VMEM((8, n_cen), F32),
        pltpu.VMEM((total, LANES), F32),
        pltpu.VMEM((total, feats), BF16),
        pltpu.VMEM((total, n_cen), BF16),
        pltpu.VMEM((slots, total), BF16),
        pltpu.VMEM((slots, feats), F32),
        pltpu.VMEM((group, n_tgt), F32),
        pltpu.VMEM((blocks, tcols, LANES), F32),
        pltpu.VMEM((n_ctr, tcols, LANES), F32),
        pltpu.VMEM((8, LANES), F32),
        pltpu.VMEM((per_block, 8, LANES), F32),
        pltpu.VMEM((tcols, LANES), BF16),
        pltpu.VMEM((blocks, tcols, LANES), BF16),
        pltpu.VMEM((panels, run, n_tgt), BF16),
        pltpu.VMEM((n_ctr, run, n_tgt), BF16),
        pltpu.VMEM((run * n_ctr, n_tgt), F32),
        pltpu.VMEM((n_pts, tcols, own_rows), F32),
        pltpu.VMEM((tcols, own_rows), BF16),
        pltpu.VMEM((owners * (panels - 1), tcols, own_rows), BF16),
        pltpu.VMEM((tcols, own_rows), BF16),
        pltpu.VMEM((owners, tcols, own_rows), BF16),
        dma((10,)), dma((n_cen // chunk,)),
        dma((n_ctr,)), dma((n_ctr,)),
        dma((n_pts,)), dma((n_pts,)),
        dma((n_ctr,)), dma((n_ctr,)),
        dma((n_ctr,)), dma((per_block,)),
        dma((blocks,)), dma((blocks,)),
        dma((n_ctr,)), dma((n_ctr,)),
        dma((n_ctr,)), dma((n_ctr,)),
        dma((n_ctr,)), dma((owners,)),
    ]
    grad, solved = pl.pallas_call(
        functools.partial(kernel, n_pts, n_ctr, panels, chunk, 256),
        out_shape=(
            pltpu.VMEM((tcols, n_cen), F32),
            pltpu.VMEM((tcols, own_rows), F32),
        ),
        in_specs=[hbm] * 10,
        out_specs=(vmem, vmem),
        scratch_shapes=scratch,
        compiler_params=pltpu.CompilerParams(
            collective_id=0, has_side_effects=True, vmem_limit_bytes=60000000
        ),
        name="falkon",
    )(
        points, point_class[None, :], targets, class_weight[None, :], inv_scale[None, :],
        index, centers, coefficients, factor, panel_inverse,
    )
    grad, solved = pl.pallas_call(
        emit,
        out_shape=(
            jax.ShapeDtypeStruct((tcols, n_cen), F32),
            jax.ShapeDtypeStruct((tcols, own_rows), F32),
        ),
        in_specs=[vmem, vmem],
        out_specs=(hbm, hbm),
        scratch_shapes=[dma((2,))],
        compiler_params=pltpu.CompilerParams(vmem_limit_bytes=1048576),
        name="emit",
    )(grad, solved)
    return grad.T, solved.T


def solution(mesh):
    placed = (
        P(("pts", "ctr"), None),
        P(("pts", "ctr")),
        P(("pts", "ctr"), None),
        P(),
        P(),
        P("ctr", None),
        P("ctr", None),
        P(),
        P("ctr", None),
        P("ctr", None),
    )
    return jax.shard_map(
        body,
        mesh=mesh,
        in_specs=placed,
        out_specs=(P("ctr", "pts"), P("ctr", "pts")),
        check_vma=False,
    )
```

time: 45.7 us -> 39.8 us (0.87)
  the two profiles are of different devices: /device:TPU:18 before, /device:TPU:22 now
where the time goes in v2:
time: 39.8 us; the launch traced here: 39.5 us
  Pallas kernels  38.9 us (98%)
  between operations  0.64 us (2%)
    pallas_call x1, Pallas kernels, body(): pl.pallas_call(functools.partial(kernel, n_pts, n_ctr, panels, chunk, 256...  38.1 us
    pallas_call x1, Pallas kernels, body(): pl.pallas_call(emit, out_shape=(jax.ShapeDtypeStruct((tcols, n_cen), F32)...  0.82 us

profile of v2, /device:TPU:22, one launch (start us, length us, event | category | flops | bytes accessed | tf_op | source)
XLA Modules:
  0.0 39.5 jit_solution(13330932319677137147)
XLA Ops:
  0.6 38.1 %falkon.1 = (f32[32,4096]{1,0:T(8,128)S(1)}, f32[32,512]{1,0:T(8,128)S(1)}) custom-call(bf16[16,512]{1,0:T(8,128)(2,1)} %pts_hbm.1, s32[1,16]{1,0:T(1,128)} %bitcast.8, f32[16,128]{1,0:T(8,128)} %tgt_hbm.1, f32[1,8]{1,0:T(1,128)} %bitcast.9, f32[1,512]{1,0:T(1,128)} %bitcast.7, s32[32,128]{1,0:T(8,128)} %bitcast.6, bf16[4096,512]{1,0:T(8,128)(2,1)} %cen_hbm.1, ...), custom_call_target="tpu_custom_call" | custom-call | tf_op jit(solution)/shard_map/falkon/pallas_call | solution.py:500
  38.7 0.8 %emit.1 = (f32[32,4096]{1,0:T(8,128)}, f32[32,512]{1,0:T(8,128)}) custom-call(f32[32,4096]{1,0:T(8,128)S(1)} %get-tuple-element.6.grad_ref, f32[32,512]{1,0:T(8,128)S(1)} %get-tuple-element.7.sol_ref), custom_call_target="tpu_custom_call" | custom-call | tf_op jit(solution)/shard_map/emit/pallas_call | solution.py:517

commit v3 on v2

--- a/solution.py
+++ b/solution.py
@@ -52,8 +52,8 @@
     pts, cls, tgt, cw, inv_row, idx, head,
     cen, coef, pinv_raw, pinv, fac_raw, fac, rnorm, pnorm, pall, kmat, ksel,
     sel, total_acc, part, part_recv, wt_send, wt_recv, rsend, rbuf,
-    wsend, wrecv, wpack, wblk, solsend, solrecv, rhssend, rhsrecv,
-    loc, cen_sem, pt_s, pt_r, fw_s, fw_r, pr_s, pr_r, wt_s, wt_r, rs_s, rs_r, w_s, w_r, so_s, so_r, rh_s, rh_r,
+    wsend, wrecv, wcount, wpack, wblk, solsend, solrecv, rhssend, rhsrecv, acc,
+    loc, cen_sem, pt_sem, fw_sem, pr_sem, wt_sem, rs_sem, w_sem, so_s, so_r, rh_s, rh_r,
 ):
     p_me, c_me = lax.axis_index("pts"), lax.axis_index("ctr")
     rows, feats = pts.shape
@@ -82,6 +82,21 @@
             device_id={"pts": p, "ctr": c}, device_id_type=MESH,
         )
 
+    def arrived(ref, sem):
+        remote(ref, ref, sem.at[0], sem.at[1], p_me, lax.rem(c_me + 1, n_ctr)).wait_recv()
+
+    def departed(ref, sem):
+        remote(ref, ref, sem.at[0], sem.at[1], p_me, lax.rem(c_me + 1, n_ctr)).wait_send()
+
+    def unless(flag, most, fn):
+        @pl.when(flag)
+        def _():
+            fn(most - 1)
+
+        @pl.when(jnp.logical_not(flag))
+        def _():
+            fn(most)
+
     def local(src, dst, k):
         return pltpu.make_async_copy(src, dst, loc.at[k])
 
@@ -105,7 +120,9 @@
     barrier = pltpu.get_barrier_semaphore()
 
     def peer(k):
-        return lax.rem(c_me + k + 1, n_ctr)
+        if n_ctr & (n_ctr - 1):
+            return lax.rem(c_me + k + 1, n_ctr)
+        return lax.bitwise_xor(c_me, jnp.where(k == 0, 1, n_ctr - k))
     pair = p_me // 2 * 2
 
     def mate(k):
@@ -149,7 +166,7 @@
 
     def pt_copy(c_src, c_dst):
         slot = pl.ds(pl.multiple_of((p_me * n_ctr + c_src) * rows, rows), rows)
-        return remote(pall.at[slot], pall.at[slot], pt_s.at[c_dst], pt_r.at[c_src], p_me, c_dst)
+        return remote(pall.at[slot], pall.at[slot], pt_sem.at[0], pt_sem.at[1], p_me, c_dst)
     each(n_ctr - 1, lambda k: pt_copy(c_me, peer(k)).start())
 
     cls_copy.wait()
@@ -169,12 +186,9 @@
         turn = lax.rem(c_me + k, per_block)
         return turn // n_pts * blocks + c_me // per_block * n_pts + lax.rem(turn, n_pts)
 
-    def wt_src(k):
-        return blk // n_pts * per_block + k
-
     def wt_copy(c_src, c_dst):
         at = lax.rem(c_src, per_block)
-        return remote(wt_send, wt_recv.at[at], wt_s.at[c_dst], wt_r.at[at], p_me, c_dst)
+        return remote(wt_send, wt_recv.at[at], wt_sem.at[0], wt_sem.at[1], p_me, c_dst)
 
     def not_me(c, fn):
         @pl.when(c != c_me)
@@ -182,7 +196,9 @@
             fn(c)
     each(per_block, lambda k: not_me(wt_dest(k), lambda c: wt_copy(c_me, c).start()))
 
-    @pl.when(c_me // per_block == blk // n_pts)
+    own_weights = c_me // per_block == blk // n_pts
+
+    @pl.when(own_weights)
     def _():
         wt_recv[lax.rem(c_me, per_block)] = weight
 
@@ -220,14 +236,14 @@
     pinv_copy.start()
     fac_copy.start()
 
-    each(n_ctr - 1, lambda k: pt_copy(peer(k), peer(k)).wait_recv())
+    arrived(pall.at[pl.ds(0, (n_ctr - 1) * rows)], pt_sem)
 
     def group_at(p):
         return pl.ds(pl.multiple_of(p * group, group), group)
 
     def fw_copy(p_src, p_dst):
         at = group_at(p_src)
-        return remote(pall.at[at], pall.at[at], fw_s.at[p_dst], fw_r.at[p_src], p_dst, c_me)
+        return remote(pall.at[at], pall.at[at], fw_sem.at[0], fw_sem.at[1], p_dst, c_me)
     for k in range(n_pts - 1):
         fw_copy(p_me, mate(k)).start()
 
@@ -239,15 +255,12 @@
     mine = pall[group_at(p_me), :]
     mine_norm = half_norm(mine)
     pnorm[group_at(p_me), :] = jnp.broadcast_to(mine_norm, (group, LANES))
-
-    def forward(k, total):
-        at = pl.ds(pl.multiple_of(k * chunk, chunk), chunk)
+    total = jnp.zeros((group, targets), F32)
+    for k in range(chunks):
+        at = pl.ds(k * chunk, chunk)
         block = kernel_block(mine, mine_norm, at)
         kmat[group_at(p_me), at] = block
-        return total + jnp.dot(block, coef[at, :], preferred_element_type=F32)
-    total = jnp.zeros((group, targets), F32)
-    for k in range(chunks):
-        total = forward(k, total)
+        total = total + jnp.dot(block, coef[at, :], preferred_element_type=F32)
     total_acc[...] = total
     own_rows_at = pl.ds(pl.multiple_of(c_me * rows, rows), rows)
     total_acc[own_rows_at, :] = total_acc[own_rows_at, :] - tgt[...]
@@ -258,7 +271,7 @@
 
     def pr_copy(c_src, c_dst):
         return remote(
-            part.at[lax.rem(c_dst, blocks)], part_recv.at[c_src], pr_s.at[c_dst], pr_r.at[c_src], p_me, c_dst
+            part.at[lax.rem(c_dst, blocks)], part_recv.at[c_src], pr_sem.at[0], pr_sem.at[1], p_me, c_dst
         )
     each(n_ctr - 1, lambda k: pr_copy(c_me, peer(k)).start())
     part_recv[c_me] = part[blk]
@@ -271,9 +284,9 @@
         sel[...] += jnp.dot(picked, cen[at, :], preferred_element_type=F32)
     each(chunks, select)
 
-    each(per_block, lambda k: not_me(wt_src(k), lambda c: wt_copy(c, c).wait_recv()))
+    unless(own_weights, per_block, lambda n: arrived(wt_recv.at[pl.ds(0, n)], wt_sem))
     weights = jnp.sum(wt_recv[...], axis=0)[0:1]
-    each(n_ctr - 1, lambda k: pr_copy(peer(k), peer(k)).wait_recv())
+    arrived(part_recv.at[pl.ds(0, n_ctr - 1)], pr_sem)
     residual = (weights * jnp.sum(part_recv[...], axis=0)).astype(BF16)
     rsend[...] = residual
 
@@ -282,29 +295,22 @@
 
     def rs_copy(p_src, b_src, p_dst, c_dst):
         at = rs_slot(p_src, b_src)
-        return remote(rsend, rbuf.at[at], rs_s.at[lax.rem(c_dst, blocks)], rs_r.at[at], p_dst, c_dst)
+        return remote(rsend, rbuf.at[at], rs_sem.at[0], rs_sem.at[1], p_dst, c_dst)
 
     def rs_out(k):
         return rs_copy(p_me, blk // n_pts, blk_pts, rep * blocks + lax.rem(blk + k, blocks))
 
-    def rs_in(k):
-        p, b, _ = source(k)
-        return rs_copy(p, b, p_me, c_me)
-
-    def rs_each(fn):
-        def step(k):
-            @pl.when(foreign(k))
-            def _():
-                fn(k)
-        each(blocks, step)
-    rs_each(lambda k: rs_out(k).start())
+    def rs_start(k):
+        @pl.when(foreign(k))
+        def _():
+            rs_out(k).start()
+    each(blocks, rs_start)
 
     @pl.when(own_block)
     def _():
         rbuf[rs_slot(p_me, blk // n_pts)] = residual
 
-    for k in range(n_pts - 1):
-        fw_copy(mate(k), mate(k)).wait_recv()
+    arrived(pall.at[pl.ds(0, (n_pts - 1) * group)], fw_sem)
     together = n_pts - 1 if group * n_pts <= 512 else 1
     for first in range(0, n_pts - 1, together):
         mates = [mate(k) for k in range(first, first + together)]
@@ -331,24 +337,42 @@
         ksel[:, at] = jnp.exp(dot_nt(chosen, pall[at, :]) - norm - chosen_norm).astype(BF16)
     each(pall.shape[0] // span, window_kernel)
 
-    rs_each(lambda k: rs_in(k).wait_recv())
+    unless(own_block, blocks, lambda n: arrived(rbuf.at[pl.ds(0, n)], rs_sem))
 
     wide_t = jnp.concatenate([rbuf[b] for b in range(blocks)], axis=1)
-    window = dot_nt(ksel[...], jnp.concatenate([wide_t] * n_pts, axis=0))
-    run = wsend.shape[1]
+    tall_t = jnp.concatenate([wide_t] * n_pts, axis=0)
+    pieces, run = wsend.shape[1], wsend.shape[2]
+    fine = pieces > 1
     lane_group = iota((run, targets), 1) // tcols
-    for panel in range(panels):
-        packed = jnp.zeros((run, targets), F32)
-        for g in range(n_pts):
-            begin = (panel * n_pts + g) * run
-            packed = packed + jnp.where(lane_group == g, window[begin:begin + run], 0.0)
-        wsend[panel] = packed.astype(BF16)
-
-    def w_copy(c_src, c_dst):
+    per_panel = slots // panels
+
+    def pack(panel):
+        window = dot_nt(ksel[panel * per_panel:(panel + 1) * per_panel], tall_t)
+        for g in range(pieces):
+            packed = jnp.zeros((run, targets), F32)
+            for h in range(n_pts):
+                begin = (g * n_pts + h) * run
+                packed = packed + jnp.where(lane_group == h, window[begin:begin + run], 0.0)
+            wsend[panel, g] = packed.astype(BF16)
+    own_piece = lax.rem(c_me, owners) * pieces // owners
+
+    def w_first(d, c_dst):
         return remote(
-            wsend.at[c_dst // owners], wrecv.at[c_src], w_s.at[c_dst], w_r.at[c_src], p_me, c_dst
+            wsend.at[0, pl.ds(0, d + 1)], wrecv.at[c_me, pl.ds(0, d + 1)], w_sem.at[0], w_sem.at[1], p_me, c_dst
         )
-    each(n_ctr - 1, lambda k: w_copy(c_me, peer(k)).start())
+
+    def w_later(c_dst):
+        d = lax.rem(c_dst, owners) * pieces // owners
+        return remote(
+            wsend.at[c_dst // owners, pl.ds(d, 1)], wrecv.at[c_me, pl.ds(d, 1)], w_sem.at[0], w_sem.at[1], p_me, c_dst
+        )
+    alike = owners // pieces
+    pack(0)
+    for d in range(pieces):
+        each(alike, lambda j: not_me(d * alike + j, lambda c: w_first(d, c).start()))
+    for panel in range(1, panels):
+        pack(panel)
+    each((panels - 1) * owners, lambda j: not_me(owners + j, lambda c: w_later(c).start()))
     wrecv[c_me] = wsend[my_panel]
 
     def backward(k):
@@ -359,65 +383,126 @@
     fac_copy.wait()
     pinv[...] = pinv_raw[...].astype(BF16)
 
-    each(n_ctr - 1, lambda k: pt_copy(c_me, peer(k)).wait_send())
-    each(per_block, lambda k: not_me(wt_dest(k), lambda c: wt_copy(c_me, c).wait_send()))
-    for k in range(n_pts - 1):
-        fw_copy(p_me, mate(k)).wait_send()
-    each(n_ctr - 1, lambda k: pr_copy(c_me, peer(k)).wait_send())
-    rs_each(lambda k: rs_out(k).wait_send())
-
-    each(n_ctr - 1, lambda k: w_copy(peer(k), peer(k)).wait_recv())
-    for o in range(n_ctr):
-        wpack[pl.ds(o, run, stride=n_ctr), :] = wrecv[head[o // wide_lanes, o % wide_lanes] // centers].astype(F32)
-
-    def so_copy(c_src, c_dst):
-        return remote(solsend, solrecv.at[c_src], so_s.at[c_dst], so_r.at[c_src], p_me, c_dst)
+    departed(pall.at[pl.ds(0, (n_ctr - 1) * rows)], pt_sem)
+    unless(own_weights, per_block, lambda n: departed(wt_recv.at[pl.ds(0, n)], wt_sem))
+    departed(pall.at[pl.ds(0, (n_pts - 1) * group)], fw_sem)
+    departed(part_recv.at[pl.ds(0, n_ctr - 1)], pr_sem)
+    unless(own_block, blocks, lambda n: departed(rbuf.at[pl.ds(0, n)], rs_sem))
+
+    w_total = sum((d + 1) * alike for d in range(pieces)) + (panels - 1) * owners
+
+    def w_departed(own):
+        departed(wcount.at[pl.ds(0, w_total - own)], w_sem)
+
+    def unpack(g):
+        for o in range(n_ctr):
+            shard = head[o // wide_lanes, o % wide_lanes] // centers
+            wpack[g, pl.ds(o, run, stride=n_ctr), :] = wrecv[shard, g].astype(F32)
+
+    halves = solsend.shape[0]
+
+    def so_copy(c_src, c_dst, h):
+        at = c_src * halves + h
+        return remote(solsend.at[h], solrecv.at[at], so_s.at[0], so_r.at[at], p_me, c_dst)
 
     def rh_copy(c_src, c_dst):
         at = lax.rem(c_src, owners)
-        return remote(rhssend, rhsrecv.at[at], rh_s.at[c_dst], rh_r.at[at], p_me, c_dst)
-
-    for panel in range(panels):
+        return remote(rhssend, rhsrecv.at[at], rh_s.at[lax.rem(c_dst, owners)], rh_r.at[at], p_me, c_dst)
+
+    half_rows = own_rows // halves
+
+    def send_solved(panel, h, result):
+        sol_ref[:, h * half_rows:(h + 1) * half_rows] = result
+        solsend[h] = result.astype(BF16)
+        later = (panels - 1 - panel) * owners
+        each(later, lambda k: so_copy(c_me, (panel + 1) * owners + k, h).start())
+
+    def departed_so(n):
+        ref = solrecv.at[pl.ds(0, n * halves)]
+        remote(ref, ref, so_s.at[0], so_r.at[0], p_me, lax.rem(c_me + 1, n_ctr)).wait_send()
+
+    def first_panel(d):
+        arrived(wrecv.at[pl.ds(0, n_ctr - 1), pl.ds(0, d + 1)], w_sem)
+        span_rows = panel_rows // (pieces * n_pts)
+        parts = []
+        for g in range(d + 1):
+            unpack(g)
+        for g in range(d + 1):
+            turned = wpack[g].T.astype(BF16)
+            parts += [turned[h * tcols:(h + 1) * tcols] for h in range(n_pts)]
+        rhs = jnp.concatenate(parts, axis=1)
+        for h in range(halves):
+            rows_at = slice(h * half_rows, (h + 1) * half_rows)
+            send_solved(0, h, dot_nt(rhs, pinv[rows_at, :(d + 1) * n_pts * span_rows]))
+        if panels > 1:
+            departed_so((panels - 1) * owners)
+        w_departed(d + 1)
+
+    for d in range(pieces):
+        @pl.when((my_panel == 0) & (own_piece == d))
+        def _():
+            first_panel(d)
+
+    for panel in range(1, panels):
         @pl.when(my_panel == panel)
         def _():
-            if panel == 0:
-                turned = wpack[...].T.astype(BF16)
-                rhs = jnp.concatenate([turned[g * tcols:(g + 1) * tcols] for g in range(n_pts)], axis=1)
+            done = panel * owners
+            position = c_me - done
+            arrived(wrecv.at[pl.ds(0, n_ctr - 1), pl.ds(0, 1)], w_sem)
+            fac[...] = fac_raw[...].astype(BF16)
+            unpack(own_piece)
+            if fine:
+                turned = wpack[own_piece].T
+                own = jnp.concatenate([turned[h * tcols:(h + 1) * tcols] for h in range(n_pts)], axis=1)
             else:
-                offset = (c_me - panel * owners) * own_rows
+                offset = position * own_rows
                 part_len = panel_rows // n_pts
                 within = pl.multiple_of(lax.rem(offset, part_len), own_rows)
-                turned = wpack[pl.ds(within, own_rows), :].T
+                turned = wpack[0, pl.ds(within, own_rows), :].T
                 for g in range(n_pts):
                     wblk[g] = turned[g * tcols:(g + 1) * tcols]
                 own = wblk[offset // part_len]
-                done = panel * owners
-                fac[...] = fac_raw[...].astype(BF16)
-                each(done, lambda k: so_copy(k, k).wait_recv())
+            if fine:
+                for b in range(done):
+                    for h in range(halves):
+                        so_copy(b, b, h).wait_recv()
+                        begin = b * own_rows + h * half_rows
+                        own = own - dot_nt(solrecv[b * halves + h], fac[:, begin:begin + half_rows])
+            else:
+                each(done, lambda k: so_copy(k, k, 0).wait_recv())
                 solved = jnp.concatenate([solrecv[b] for b in range(done)], axis=1)
                 own = own - dot_nt(solved, fac[:, :done * own_rows])
-                rhssend[...] = own.astype(BF16)
-
-                def fellow(k):
-                    return panel * owners + lax.rem(c_me - panel * owners + k + 1, owners)
-                each(owners - 1, lambda k: rh_copy(c_me, fellow(k)).start())
-                rhsrecv[c_me - panel * owners] = rhssend[...]
-                each(owners - 1, lambda k: rh_copy(fellow(k), fellow(k)).wait_recv())
-                rhs = jnp.concatenate([rhsrecv[b] for b in range(owners)], axis=1)
-            result = dot_nt(rhs, pinv[...])
-            sol_ref[...] = result
+            rhssend[...] = own.astype(BF16)
+
+            def below(k, fn):
+                @pl.when(k > position if fine else k != position)
+                def _():
+                    fn(done + k)
+            each(owners, lambda k: below(owners - 1 - k, lambda c: rh_copy(c_me, c).start()))
+            if fine:
+                acc[...] = jnp.zeros_like(acc)
+                rhsrecv[position] = rhssend[...]
+                for b in range(owners):
+                    @pl.when(b <= position)
+                    def _():
+                        @pl.when(b < position)
+                        def _():
+                            rh_copy(done + b, done + b).wait_recv()
+                        acc[...] += dot_nt(rhsrecv[b], pinv[:, b * own_rows:(b + 1) * own_rows])
+                result = acc[...]
+            else:
+                rhsrecv[position] = rhssend[...]
+                each(owners, lambda k: below(k, lambda c: rh_copy(c, c).wait_recv()))
+                result = dot_nt(jnp.concatenate([rhsrecv[b] for b in range(owners)], axis=1), pinv[...])
             later = (panels - 1 - panel) * owners
             if later:
-                solsend[...] = result.astype(BF16)
-
-                def after(k):
-                    return (panel + 1) * owners + lax.rem(k + c_me, later)
-                each(later, lambda k: so_copy(c_me, after(k)).start())
-                each(later, lambda k: so_copy(c_me, after(k)).wait_send())
-            if panel > 0:
-                each(owners - 1, lambda k: rh_copy(c_me, fellow(k)).wait_send())
-
-    each(n_ctr - 1, lambda k: w_copy(c_me, peer(k)).wait_send())
+                for h in range(halves):
+                    send_solved(panel, h, result[:, h * half_rows:(h + 1) * half_rows])
+                departed_so(later)
+            else:
+                sol_ref[...] = result
+            each(owners, lambda k: below(k, lambda c: rh_copy(c_me, c).wait_send()))
+            w_departed(1)
 
 
 def emit(grad_ref, sol_ref, grad_out, sol_out, sem):
@@ -445,7 +530,10 @@
     pt_blocks = n_ctr // per_block
     blocks = n_pts * pt_blocks
     slots = center_index.shape[0] // n_ctr
-    run = slots // panels // n_pts
+    pieces = owners if own_rows % LANES == 0 else 1
+    halves = 1
+    run = slots // panels // pieces // n_pts
+    w_most = pieces * (pieces + 1) // 2 * (owners // pieces) + (panels - 1) * owners
     solved_cols = panel_rows * (panels - 1)
     chunk = 1024
     index = center_index.reshape(-1, LANES)
@@ -479,23 +567,20 @@
         pltpu.VMEM((per_block, 8, LANES), F32),
         pltpu.VMEM((tcols, LANES), BF16),
         pltpu.VMEM((blocks, tcols, LANES), BF16),
-        pltpu.VMEM((panels, run, n_tgt), BF16),
-        pltpu.VMEM((n_ctr, run, n_tgt), BF16),
-        pltpu.VMEM((run * n_ctr, n_tgt), F32),
+        pltpu.VMEM((panels, pieces, run, n_tgt), BF16),
+        pltpu.VMEM((n_ctr, pieces, run, n_tgt), BF16),
+        pltpu.VMEM((w_most, run, n_tgt), BF16),
+        pltpu.VMEM((pieces, run * n_ctr, n_tgt), F32),
         pltpu.VMEM((n_pts, tcols, own_rows), F32),
-        pltpu.VMEM((tcols, own_rows), BF16),
-        pltpu.VMEM((owners * (panels - 1), tcols, own_rows), BF16),
+        pltpu.VMEM((halves, tcols, own_rows // halves), BF16),
+        pltpu.VMEM((owners * (panels - 1) * halves, tcols, own_rows // halves), BF16),
         pltpu.VMEM((tcols, own_rows), BF16),
         pltpu.VMEM((owners, tcols, own_rows), BF16),
+        pltpu.VMEM((tcols, own_rows), F32),
         dma((10,)), dma((n_cen // chunk,)),
-        dma((n_ctr,)), dma((n_ctr,)),
-        dma((n_pts,)), dma((n_pts,)),
-        dma((n_ctr,)), dma((n_ctr,)),
-        dma((n_ctr,)), dma((per_block,)),
-        dma((blocks,)), dma((blocks,)),
-        dma((n_ctr,)), dma((n_ctr,)),
-        dma((n_ctr,)), dma((n_ctr,)),
-        dma((n_ctr,)), dma((owners,)),
+        dma((2,)), dma((2,)), dma((2,)), dma((2,)), dma((2,)), dma((2,)),
+        dma((1,)), dma((owners * (panels - 1) * halves,)),
+        dma((owners,)), dma((owners,)),
     ]
     grad, solved = pl.pallas_call(
         functools.partial(kernel, n_pts, n_ctr, panels, chunk, 256),

time: 39.8 us -> 36 us (0.905)
  the two profiles are of different devices: /device:TPU:22 before, /device:TPU:26 now
where the time goes in v3:
time: 36 us; the launch traced here: 35.4 us
  Pallas kernels  34.8 us (97%)
  between operations  0.64 us (2%)
    pallas_call x1, Pallas kernels, body(): pl.pallas_call(functools.partial(kernel, n_pts, n_ctr, panels, chunk, 256...  33.9 us
    pallas_call x1, Pallas kernels, body(): pl.pallas_call(emit, out_shape=(jax.ShapeDtypeStruct((tcols, n_cen), F32)...  0.82 us

profile of v3, /device:TPU:26, one launch (start us, length us, event | category | flops | bytes accessed | tf_op | source)
XLA Modules:
  0.0 35.4 jit_solution(6603722785940235249)
XLA Ops:
  0.6 33.9 %falkon.1 = (f32[32,4096]{1,0:T(8,128)S(1)}, f32[32,512]{1,0:T(8,128)S(1)}) custom-call(bf16[16,512]{1,0:T(8,128)(2,1)} %pts_hbm.1, s32[1,16]{1,0:T(1,128)} %bitcast.8, f32[16,128]{1,0:T(8,128)} %tgt_hbm.1, f32[1,8]{1,0:T(1,128)} %bitcast.9, f32[1,512]{1,0:T(1,128)} %bitcast.7, s32[32,128]{1,0:T(8,128)} %bitcast.6, bf16[4096,512]{1,0:T(8,128)(2,1)} %cen_hbm.1, ...), custom_call_target="tpu_custom_call" | custom-call | tf_op jit(solution)/shard_map/falkon/pallas_call | solution.py:585
  34.6 0.8 %emit.1 = (f32[32,4096]{1,0:T(8,128)}, f32[32,512]{1,0:T(8,128)}) custom-call(f32[32,4096]{1,0:T(8,128)S(1)} %get-tuple-element.6.grad_ref, f32[32,512]{1,0:T(8,128)S(1)} %get-tuple-element.7.sol_ref), custom_call_target="tpu_custom_call" | custom-call | tf_op jit(solution)/shard_map/emit/pallas_call | solution.py:602

commit v4 on v3

--- a/solution.py
+++ b/solution.py
@@ -45,13 +45,20 @@
     lax.fori_loop(0, n, step, 0)
 
 
+def unrolled(n, fn):
+    if n > 8:
+        return each(n, fn)
+    for k in range(n):
+        fn(k)
+
+
 def kernel(
     n_pts, n_ctr, panels, chunk, sub,
     pts_hbm, cls_hbm, tgt_hbm, cw_hbm, inv_hbm, idx_hbm, cen_hbm, coef_hbm, fac_hbm, pinv_hbm,
     grad_ref, sol_ref,
     pts, cls, tgt, cw, inv_row, idx, head,
     cen, coef, pinv_raw, pinv, fac_raw, fac, rnorm, pnorm, pall, kmat, ksel,
-    sel, total_acc, part, part_recv, wt_send, wt_recv, rsend, rbuf,
+    sel, total_acc, part, part_recv, wt_send, wt_recv, rsend, rbuf, rcount,
     wsend, wrecv, wcount, wpack, wblk, solsend, solrecv, rhssend, rhsrecv, acc,
     loc, cen_sem, pt_sem, fw_sem, pr_sem, wt_sem, rs_sem, w_sem, so_s, so_r, rh_s, rh_r,
 ):
@@ -68,13 +75,13 @@
     blocks = rbuf.shape[0]
     pt_blocks = blocks // n_pts
     per_block = n_ctr // pt_blocks
-    copies = n_ctr // blocks
     width = rows * per_block
     me = p_me * n_ctr + c_me
-    blk = lax.rem(c_me, blocks)
-    rep = c_me // blocks
-    blk_pts = lax.rem(blk, n_pts)
-    own_block = blk_pts == p_me
+    first_red = (n_ctr - blocks) // 2
+    reduces = (c_me >= first_red) & (c_me < first_red + blocks)
+    blk = jnp.where(reduces, c_me - first_red, 0)
+    blk_pts = lax.rem(blk + p_me // 2 * 2, n_pts)
+    own_block = reduces & (blk_pts == p_me)
 
     def remote(src, dst, send, recv, p, c):
         return pltpu.make_async_remote_copy(
@@ -120,35 +127,22 @@
     barrier = pltpu.get_barrier_semaphore()
 
     def peer(k):
-        if n_ctr & (n_ctr - 1):
-            return lax.rem(c_me + k + 1, n_ctr)
-        return lax.bitwise_xor(c_me, jnp.where(k == 0, 1, n_ctr - k))
+        above = n_ctr - 1 - c_me
+        low = jnp.where(k < above, n_ctr - 1 - k, k - above)
+        high = jnp.where(k < c_me, k, n_ctr - 1 - k + c_me)
+        return jnp.where(c_me < above, low, high)
     pair = p_me // 2 * 2
 
     def mate(k):
         return 2 * pair + 1 - p_me if k == 0 else lax.rem(pair + k + 1, n_pts)
 
-    def source(k):
-        p = lax.rem(p_me + k, n_pts)
-        b = lax.rem(blk // n_pts + k // n_pts, pt_blocks)
-        return p, b, rep * blocks + b * n_pts + p_me
-
     def greet(p, c):
         pl.semaphore_signal(barrier, inc=1, device_id={"pts": p, "ctr": c}, device_id_type=MESH)
-
-    def foreign(k):
-        return jnp.logical_or(k != 0, jnp.logical_not(own_block))
 
     each(n_ctr - 1, lambda k: greet(p_me, peer(k)))
     for k in range(n_pts - 1):
         greet(mate(k), c_me)
 
-    def greet_source(k):
-        @pl.when(foreign(k))
-        def _():
-            p, _, c = source(k)
-            greet(p, c)
-    each(blocks, greet_source)
     cls_copy.start()
     cw_copy.start()
     each(chunks, lambda k: cen_copy(k).start())
@@ -162,7 +156,7 @@
     inv = inv_row[...]
     own_slot = pl.ds(pl.multiple_of(me * rows, rows), rows)
     pall[own_slot, :] = (pts[...].astype(F32) * inv).astype(BF16)
-    pl.semaphore_wait(barrier, n_ctr + n_pts - 2 + blocks - own_block.astype(jnp.int32))
+    pl.semaphore_wait(barrier, n_ctr + n_pts - 2)
 
     def pt_copy(c_src, c_dst):
         slot = pl.ds(pl.multiple_of((p_me * n_ctr + c_src) * rows, rows), rows)
@@ -183,8 +177,7 @@
     wt_send[...] = weight
 
     def wt_dest(k):
-        turn = lax.rem(c_me + k, per_block)
-        return turn // n_pts * blocks + c_me // per_block * n_pts + lax.rem(turn, n_pts)
+        return first_red + c_me // per_block * n_pts + k
 
     def wt_copy(c_src, c_dst):
         at = lax.rem(c_src, per_block)
@@ -194,9 +187,9 @@
         @pl.when(c != c_me)
         def _():
             fn(c)
-    each(per_block, lambda k: not_me(wt_dest(k), lambda c: wt_copy(c_me, c).start()))
-
-    own_weights = c_me // per_block == blk // n_pts
+    each(n_pts, lambda k: not_me(wt_dest(k), lambda c: wt_copy(c_me, c).start()))
+
+    own_weights = reduces & (c_me // per_block == blk // n_pts)
 
     @pl.when(own_weights)
     def _():
@@ -212,7 +205,7 @@
 
     def scale_chunk(k):
         cen_copy(k).wait()
-        each(chunk // step, lambda j: scale(k * (chunk // step) + j))
+        unrolled(chunk // step, lambda j: scale(k * (chunk // step) + j))
     each(chunks, scale_chunk)
 
     idx_copy.wait()
@@ -269,48 +262,53 @@
         for q in range(n_pts):
             part[b * n_pts + q] = turned[q * tcols:(q + 1) * tcols]
 
+    def part_of(b):
+        return b // n_pts * n_pts + lax.rem(b + p_me // 2 * 2, n_pts)
+
     def pr_copy(c_src, c_dst):
         return remote(
-            part.at[lax.rem(c_dst, blocks)], part_recv.at[c_src], pr_sem.at[0], pr_sem.at[1], p_me, c_dst
+            part.at[part_of(c_dst - first_red)], part_recv.at[c_src], pr_sem.at[0], pr_sem.at[1], p_me, c_dst
         )
-    each(n_ctr - 1, lambda k: pr_copy(c_me, peer(k)).start())
-    part_recv[c_me] = part[blk]
+    def pr_dest(k):
+        return jnp.where(c_me < n_ctr // 2, first_red + blocks - 1 - k, first_red + k)
+    each(blocks, lambda k: not_me(pr_dest(k), lambda c: pr_copy(c_me, c).start()))
+    part_recv[c_me] = part[part_of(blk)]
 
     sel[...] = jnp.zeros_like(sel)
 
     def select(k):
         at = pl.ds(pl.multiple_of(k * chunk, chunk), chunk)
         picked = hot(iota((slots, chunk), 1) == local_row - k * chunk)
-        sel[...] += jnp.dot(picked, cen[at, :], preferred_element_type=F32)
-    each(chunks, select)
-
-    unless(own_weights, per_block, lambda n: arrived(wt_recv.at[pl.ds(0, n)], wt_sem))
-    weights = jnp.sum(wt_recv[...], axis=0)[0:1]
-    arrived(part_recv.at[pl.ds(0, n_ctr - 1)], pr_sem)
-    residual = (weights * jnp.sum(part_recv[...], axis=0)).astype(BF16)
-    rsend[...] = residual
+        return jnp.dot(picked, cen[at, :], preferred_element_type=F32)
+    sel[...] = functools.reduce(lambda a, k: a + select(k), range(1, chunks), select(0))
+
+    arrived(pall.at[pl.ds(0, (n_pts - 1) * group)], fw_sem)
 
     def rs_slot(p, b):
         return p * pt_blocks + b
 
-    def rs_copy(p_src, b_src, p_dst, c_dst):
-        at = rs_slot(p_src, b_src)
-        return remote(rsend, rbuf.at[at], rs_sem.at[0], rs_sem.at[1], p_dst, c_dst)
-
-    def rs_out(k):
-        return rs_copy(p_me, blk // n_pts, blk_pts, rep * blocks + lax.rem(blk + k, blocks))
-
-    def rs_start(k):
-        @pl.when(foreign(k))
+    def rs_copy(c_dst):
+        at = rs_slot(p_me, blk // n_pts)
+        return remote(rsend, rbuf.at[at], rs_sem.at[0], rs_sem.at[1], blk_pts, c_dst)
+
+    @pl.when(reduces)
+    def _():
+        unless(own_weights, per_block, lambda n: arrived(wt_recv.at[pl.ds(0, n)], wt_sem))
+        weights = jnp.sum(wt_recv[...], axis=0)[0:1]
+        arrived(part_recv.at[pl.ds(0, n_ctr - 1)], pr_sem)
+        residual = (weights * jnp.sum(part_recv[...], axis=0)).astype(BF16)
+        rsend[...] = residual
+
+        @pl.when(own_block)
         def _():
-            rs_out(k).start()
-    each(blocks, rs_start)
-
-    @pl.when(own_block)
-    def _():
-        rbuf[rs_slot(p_me, blk // n_pts)] = residual
-
-    arrived(pall.at[pl.ds(0, (n_pts - 1) * group)], fw_sem)
+            rbuf[rs_slot(p_me, blk // n_pts)] = residual
+            each(n_ctr - 1, lambda k: rs_copy(peer(k)).start())
+
+        @pl.when(jnp.logical_not(own_block))
+        def _():
+            each(n_ctr - 1, lambda k: rs_copy(peer(k)).start())
+            rs_copy(c_me).start()
+
     together = n_pts - 1 if group * n_pts <= 512 else 1
     for first in range(0, n_pts - 1, together):
         mates = [mate(k) for k in range(first, first + together)]
@@ -325,7 +323,7 @@
                 block = kernel_block(left, left_norm, at)
                 for n, p in enumerate(mates):
                     kmat[group_at(p), at] = block[n * group:(n + 1) * group]
-        each(chunks, fill)
+        unrolled(chunks, fill)
 
     chosen = sel[...].astype(BF16)
     chosen_norm = half_norm(chosen)
@@ -378,16 +376,19 @@
     def backward(k):
         at = pl.ds(pl.multiple_of(k * chunk, chunk), chunk)
         grad_ref[:, at] = jnp.dot(wide_t, kmat[:, at], preferred_element_type=F32)
-    each(chunks, backward)
+    unrolled(chunks, backward)
     pinv_copy.wait()
     fac_copy.wait()
     pinv[...] = pinv_raw[...].astype(BF16)
 
     departed(pall.at[pl.ds(0, (n_ctr - 1) * rows)], pt_sem)
-    unless(own_weights, per_block, lambda n: departed(wt_recv.at[pl.ds(0, n)], wt_sem))
+    unless(own_weights, n_pts, lambda n: departed(wt_recv.at[pl.ds(0, n)], wt_sem))
     departed(pall.at[pl.ds(0, (n_pts - 1) * group)], fw_sem)
-    departed(part_recv.at[pl.ds(0, n_ctr - 1)], pr_sem)
-    unless(own_block, blocks, lambda n: departed(rbuf.at[pl.ds(0, n)], rs_sem))
+    unless(reduces, blocks, lambda n: departed(part.at[pl.ds(0, n)], pr_sem))
+
+    @pl.when(reduces)
+    def _():
+        unless(own_block, n_ctr, lambda n: departed(rcount.at[pl.ds(0, n)], rs_sem))
 
     w_total = sum((d + 1) * alike for d in range(pieces)) + (panels - 1) * owners
 
@@ -567,6 +568,7 @@
         pltpu.VMEM((per_block, 8, LANES), F32),
         pltpu.VMEM((tcols, LANES), BF16),
         pltpu.VMEM((blocks, tcols, LANES), BF16),
+        pltpu.VMEM((n_ctr, tcols, LANES), BF16),
         pltpu.VMEM((panels, pieces, run, n_tgt), BF16),
         pltpu.VMEM((n_ctr, pieces, run, n_tgt), BF16),
         pltpu.VMEM((w_most, run, n_tgt), BF16),
@@ -583,7 +585,7 @@
         dma((owners,)), dma((owners,)),
     ]
     grad, solved = pl.pallas_call(
-        functools.partial(kernel, n_pts, n_ctr, panels, chunk, 256),
+        functools.partial(kernel, n_pts, n_ctr, panels, chunk, 512),
         out_shape=(
             pltpu.VMEM((tcols, n_cen), F32),
             pltpu.VMEM((tcols, own_rows), F32),

time: 36 us -> 34.6 us (0.961)
  Pallas kernels: 34.8 us -> 33.7 us
    pallas_call x1, Pallas kernels: 33.9 us -> 32.9 us  [body(): pl.pallas_call(functools.partial(kernel, n_pts, n_ctr, panels, chunk, 512...]
where the time goes in v4:
time: 34.6 us; the launch traced here: 34.4 us
  Pallas kernels  33.7 us (97%)
  between operations  0.64 us (2%)
    pallas_call x1, Pallas kernels, body(): pl.pallas_call(functools.partial(kernel, n_pts, n_ctr, panels, chunk, 512...  32.9 us
    pallas_call x1, Pallas kernels, body(): pl.pallas_call(emit, out_shape=(jax.ShapeDtypeStruct((tcols, n_cen), F32)...  0.82 us

profile of v4, /device:TPU:26, one launch (start us, length us, event | category | flops | bytes accessed | tf_op | source)
XLA Modules:
  0.0 34.4 jit_solution(3320111484872835369)
XLA Ops:
  0.6 32.9 %falkon.1 = (f32[32,4096]{1,0:T(8,128)S(1)}, f32[32,512]{1,0:T(8,128)S(1)}) custom-call(bf16[16,512]{1,0:T(8,128)(2,1)} %pts_hbm.1, s32[1,16]{1,0:T(1,128)} %bitcast.8, f32[16,128]{1,0:T(8,128)} %tgt_hbm.1, f32[1,8]{1,0:T(1,128)} %bitcast.9, f32[1,512]{1,0:T(1,128)} %bitcast.7, s32[32,128]{1,0:T(8,128)} %bitcast.6, bf16[4096,512]{1,0:T(8,128)(2,1)} %cen_hbm.1, ...), custom_call_target="tpu_custom_call" | custom-call | tf_op jit(solution)/shard_map/falkon/pallas_call | solution.py:587
  33.5 0.8 %emit.1 = (f32[32,4096]{1,0:T(8,128)}, f32[32,512]{1,0:T(8,128)}) custom-call(f32[32,4096]{1,0:T(8,128)S(1)} %get-tuple-element.6.grad_ref, f32[32,512]{1,0:T(8,128)S(1)} %get-tuple-element.7.sol_ref), custom_call_target="tpu_custom_call" | custom-call | tf_op jit(solution)/shard_map/emit/pallas_call | solution.py:604

commit v5 on v4

--- a/solution.py
+++ b/solution.py
@@ -59,8 +59,8 @@
     pts, cls, tgt, cw, inv_row, idx, head,
     cen, coef, pinv_raw, pinv, fac_raw, fac, rnorm, pnorm, pall, kmat, ksel,
     sel, total_acc, part, part_recv, wt_send, wt_recv, rsend, rbuf, rcount,
-    wsend, wrecv, wcount, wpack, wblk, solsend, solrecv, rhssend, rhsrecv, acc,
-    loc, cen_sem, pt_sem, fw_sem, pr_sem, wt_sem, rs_sem, w_sem, so_s, so_r, rh_s, rh_r,
+    wsend, wrecv, wcount, wsend_t, wrecv_t, tall, mixed, wpack, wblk, solsend, solrecv, rhssend, rhsrecv, acc,
+    loc, cen_sem, pt_sem, fw_sem, pr_sem, wt_sem, rs_sem, w0_sem, w_sem, so_s, so_r, rh_s, rh_r,
 ):
     p_me, c_me = lax.axis_index("pts"), lax.axis_index("ctr")
     rows, feats = pts.shape
@@ -249,10 +249,16 @@
     mine_norm = half_norm(mine)
     pnorm[group_at(p_me), :] = jnp.broadcast_to(mine_norm, (group, LANES))
     total = jnp.zeros((group, targets), F32)
+    saved = []
     for k in range(chunks):
         at = pl.ds(k * chunk, chunk)
         block = kernel_block(mine, mine_norm, at)
         kmat[group_at(p_me), at] = block
+        if group > LANES:
+            total = total + jnp.dot(block, coef[at, :], preferred_element_type=F32)
+        else:
+            saved.append((block, at))
+    for block, at in saved:
         total = total + jnp.dot(block, coef[at, :], preferred_element_type=F32)
     total_acc[...] = total
     own_rows_at = pl.ds(pl.multiple_of(c_me * rows, rows), rows)
@@ -365,13 +371,34 @@
             wsend.at[c_dst // owners, pl.ds(d, 1)], wrecv.at[c_me, pl.ds(d, 1)], w_sem.at[0], w_sem.at[1], p_me, c_dst
         )
     alike = owners // pieces
-    pack(0)
+    lane_parts = wsend_t.shape[0]
+
+    def reach(d):
+        return ((d + 1) * lane_parts + pieces - 1) // pieces
+
+    def wt_first(d, c_src, c_dst):
+        at = pl.ds(0, reach(d))
+        return remote(wsend_t.at[at], wrecv_t.at[c_src, at], w0_sem.at[0], w0_sem.at[1 + c_src], p_me, c_dst)
+    if fine:
+        turned = dot_nt(wide_t, ksel[:per_panel]).astype(BF16)
+        for g in range(lane_parts):
+            wsend_t[g] = turned[:, g * LANES:(g + 1) * LANES]
+    else:
+        pack(0)
     for d in range(pieces):
-        each(alike, lambda j: not_me(d * alike + j, lambda c: w_first(d, c).start()))
+        send = functools.partial(wt_first, d, c_me) if fine else functools.partial(w_first, d)
+        each(alike, lambda j: not_me(d * alike + j, lambda c: send(c).start()))
+    if fine:
+        wrecv_t[c_me] = wsend_t[...]
     for panel in range(1, panels):
         pack(panel)
     each((panels - 1) * owners, lambda j: not_me(owners + j, lambda c: w_later(c).start()))
-    wrecv[c_me] = wsend[my_panel]
+    if not fine:
+        wrecv[c_me] = wsend[my_panel]
+    else:
+        @pl.when(my_panel > 0)
+        def _():
+            wrecv[c_me] = wsend[my_panel]
 
     def backward(k):
         at = pl.ds(pl.multiple_of(k * chunk, chunk), chunk)
@@ -379,7 +406,21 @@
     unrolled(chunks, backward)
     pinv_copy.wait()
     fac_copy.wait()
-    pinv[...] = pinv_raw[...].astype(BF16)
+    if fine:
+        @pl.when(my_panel > 0)
+        def _():
+            pinv[...] = pinv_raw[...].astype(BF16)
+
+        @pl.when(my_panel == 0)
+        def _():
+            for g in range(own_rows // LANES):
+                rows_at = slice(g * LANES, (g + 1) * LANES)
+                for begin in range(0, panel_rows, LANES):
+                    tall[g, begin:begin + LANES] = pinv_raw[rows_at, begin:begin + LANES].T
+                for o in range(n_ctr):
+                    mixed[o, :, rows_at] = tall[g, pl.ds(o, per_panel, stride=n_ctr), :].astype(BF16)
+    else:
+        pinv[...] = pinv_raw[...].astype(BF16)
 
     departed(pall.at[pl.ds(0, (n_ctr - 1) * rows)], pt_sem)
     unless(own_weights, n_pts, lambda n: departed(wt_recv.at[pl.ds(0, n)], wt_sem))
@@ -390,10 +431,15 @@
     def _():
         unless(own_block, n_ctr, lambda n: departed(rcount.at[pl.ds(0, n)], rs_sem))
 
-    w_total = sum((d + 1) * alike for d in range(pieces)) + (panels - 1) * owners
-
-    def w_departed(own):
-        departed(wcount.at[pl.ds(0, w_total - own)], w_sem)
+    w_ahead = sum((d + 1) * alike for d in range(pieces))
+    w_after = (panels - 1) * owners
+
+    def w_departed(own, panel):
+        if fine:
+            departed(rcount.at[pl.ds(0, sum(reach(d) for d in range(pieces)) - (reach(own) if panel == 0 else 0))], w0_sem)
+            departed(wcount.at[pl.ds(0, w_after - (panel > 0))], w_sem)
+        else:
+            departed(wcount.at[pl.ds(0, w_ahead + w_after - (own + 1 if panel == 0 else 1))], w_sem)
 
     def unpack(g):
         for o in range(n_ctr):
@@ -423,21 +469,32 @@
         remote(ref, ref, so_s.at[0], so_r.at[0], p_me, lax.rem(c_me + 1, n_ctr)).wait_send()
 
     def first_panel(d):
-        arrived(wrecv.at[pl.ds(0, n_ctr - 1), pl.ds(0, d + 1)], w_sem)
-        span_rows = panel_rows // (pieces * n_pts)
-        parts = []
-        for g in range(d + 1):
-            unpack(g)
-        for g in range(d + 1):
-            turned = wpack[g].T.astype(BF16)
-            parts += [turned[h * tcols:(h + 1) * tcols] for h in range(n_pts)]
-        rhs = jnp.concatenate(parts, axis=1)
-        for h in range(halves):
-            rows_at = slice(h * half_rows, (h + 1) * half_rows)
-            send_solved(0, h, dot_nt(rhs, pinv[rows_at, :(d + 1) * n_pts * span_rows]))
+        if fine:
+            depth = reach(d) * LANES
+            result = jnp.zeros((tcols, own_rows), F32)
+            for k in range(n_ctr - 1, -1, -1):
+                source = c_me if k == n_ctr - 1 else peer(k)
+                if k < n_ctr - 1:
+                    wt_first(d, source, source).wait_recv()
+                spot = 0
+                for o in range(1, n_ctr):
+                    spot = jnp.where(head[o // wide_lanes, o % wide_lanes] // centers == source, o, spot)
+                left = jnp.concatenate([wrecv_t[source, g] for g in range(reach(d))], axis=1)
+                result = result + jnp.dot(left, mixed[spot, :depth], preferred_element_type=F32)
+            send_solved(0, 0, result)
+        else:
+            arrived(wrecv.at[pl.ds(0, n_ctr - 1), pl.ds(0, d + 1)], w_sem)
+            for g in range(d + 1):
+                unpack(g)
+            parts = []
+            for g in range(d + 1):
+                turned = wpack[g].T.astype(BF16)
+                parts += [turned[h * tcols:(h + 1) * tcols] for h in range(n_pts)]
+            rhs = jnp.concatenate(parts, axis=1)
+            send_solved(0, 0, dot_nt(rhs, pinv[:, :(d + 1) * (panel_rows // pieces)]))
         if panels > 1:
             departed_so((panels - 1) * owners)
-        w_departed(d + 1)
+        w_departed(d, 0)
 
     for d in range(pieces):
         @pl.when((my_panel == 0) & (own_piece == d))
@@ -503,7 +560,7 @@
             else:
                 sol_ref[...] = result
             each(owners, lambda k: below(k, lambda c: rh_copy(c_me, c).wait_send()))
-            w_departed(1)
+            w_departed(0, panel)
 
 
 def emit(grad_ref, sol_ref, grad_out, sol_out, sem):
@@ -533,6 +590,7 @@
     slots = center_index.shape[0] // n_ctr
     pieces = owners if own_rows % LANES == 0 else 1
     halves = 1
+    lane_parts = max(1, slots // panels // LANES)
     run = slots // panels // pieces // n_pts
     w_most = pieces * (pieces + 1) // 2 * (owners // pieces) + (panels - 1) * owners
     solved_cols = panel_rows * (panels - 1)
@@ -572,6 +630,10 @@
         pltpu.VMEM((panels, pieces, run, n_tgt), BF16),
         pltpu.VMEM((n_ctr, pieces, run, n_tgt), BF16),
         pltpu.VMEM((w_most, run, n_tgt), BF16),
+        pltpu.VMEM((lane_parts, tcols, LANES), BF16),
+        pltpu.VMEM((n_ctr, lane_parts, tcols, LANES), BF16),
+        pltpu.VMEM((max(1, own_rows // LANES), panel_rows, LANES), F32),
+        pltpu.VMEM((n_ctr, slots // panels, own_rows), BF16),
         pltpu.VMEM((pieces, run * n_ctr, n_tgt), F32),
         pltpu.VMEM((n_pts, tcols, own_rows), F32),
         pltpu.VMEM((halves, tcols, own_rows // halves), BF16),
@@ -580,7 +642,7 @@
         pltpu.VMEM((owners, tcols, own_rows), BF16),
         pltpu.VMEM((tcols, own_rows), F32),
         dma((10,)), dma((n_cen // chunk,)),
-        dma((2,)), dma((2,)), dma((2,)), dma((2,)), dma((2,)), dma((2,)),
+        dma((2,)), dma((2,)), dma((2,)), dma((2,)), dma((2,)), dma((1 + n_ctr,)), dma((2,)),
         dma((1,)), dma((owners * (panels - 1) * halves,)),
         dma((owners,)), dma((owners,)),
     ]

time: 34.6 us -> 34.4 us (level)
  no operation moved by 1% of the time
where the time goes in v5:
time: 34.4 us; the launch traced here: 34.1 us
  Pallas kernels  33.5 us (97%)
  between operations  0.64 us (2%)
    pallas_call x1, Pallas kernels, body(): pl.pallas_call(functools.partial(kernel, n_pts, n_ctr, panels, chunk, 512...  32.6 us
    pallas_call x1, Pallas kernels, body(): pl.pallas_call(emit, out_shape=(jax.ShapeDtypeStruct((tcols, n_cen), F32)...  0.82 us

profile of v5, /device:TPU:26, one launch (start us, length us, event | category | flops | bytes accessed | tf_op | source)
XLA Modules:
  0.0 34.1 jit_solution(14764029182404033017)
XLA Ops:
  0.6 32.6 %falkon.1 = (f32[32,4096]{1,0:T(8,128)S(1)}, f32[32,512]{1,0:T(8,128)S(1)}) custom-call(bf16[16,512]{1,0:T(8,128)(2,1)} %pts_hbm.1, s32[1,16]{1,0:T(1,128)} %bitcast.8, f32[16,128]{1,0:T(8,128)} %tgt_hbm.1, f32[1,8]{1,0:T(1,128)} %bitcast.9, f32[1,512]{1,0:T(1,128)} %bitcast.7, s32[32,128]{1,0:T(8,128)} %bitcast.6, bf16[4096,512]{1,0:T(8,128)(2,1)} %cen_hbm.1, ...), custom_call_target="tpu_custom_call" | custom-call | tf_op jit(solution)/shard_map/falkon/pallas_call | solution.py:649
  33.3 0.8 %emit.1 = (f32[32,4096]{1,0:T(8,128)}, f32[32,512]{1,0:T(8,128)}) custom-call(f32[32,4096]{1,0:T(8,128)S(1)} %get-tuple-element.6.grad_ref, f32[32,512]{1,0:T(8,128)S(1)} %get-tuple-element.7.sol_ref), custom_call_target="tpu_custom_call" | custom-call | tf_op jit(solution)/shard_map/emit/pallas_call | solution.py:666

commit v6 on v5

--- a/solution.py
+++ b/solution.py
@@ -448,9 +448,9 @@
 
     halves = solsend.shape[0]
 
-    def so_copy(c_src, c_dst, h):
+    def so_copy(c_src, c_dst, h, late=0):
         at = c_src * halves + h
-        return remote(solsend.at[h], solrecv.at[at], so_s.at[0], so_r.at[at], p_me, c_dst)
+        return remote(solsend.at[h], solrecv.at[at], so_s.at[late], so_r.at[at], p_me, c_dst)
 
     def rh_copy(c_src, c_dst):
         at = lax.rem(c_src, owners)
@@ -462,11 +462,26 @@
         sol_ref[:, h * half_rows:(h + 1) * half_rows] = result
         solsend[h] = result.astype(BF16)
         later = (panels - 1 - panel) * owners
-        each(later, lambda k: so_copy(c_me, (panel + 1) * owners + k, h).start())
-
-    def departed_so(n):
+        ahead = later // 2
+        held = 1 if fine and later else 0
+        each(ahead, lambda k: so_copy(c_me, (panel + 1) * owners + k, h).start())
+        each(later - ahead - held, lambda k: so_copy(c_me, (panel + 1) * owners + ahead + k, h, 1).start())
+        if held:
+            departed_so(ahead, 0)
+
+            @pl.when(c_me < owners // 2)
+            def _():
+                pl.delay(2500)
+            so_copy(c_me, n_ctr - 1, h, 1).start()
+
+    def departed_so(n, late):
         ref = solrecv.at[pl.ds(0, n * halves)]
-        remote(ref, ref, so_s.at[0], so_r.at[0], p_me, lax.rem(c_me + 1, n_ctr)).wait_send()
+        remote(ref, ref, so_s.at[late], so_r.at[0], p_me, lax.rem(c_me + 1, n_ctr)).wait_send()
+
+    def departed_rest(n):
+        if not fine:
+            departed_so(n // 2, 0)
+        departed_so(n - n // 2, 1)
 
     def first_panel(d):
         if fine:
@@ -493,7 +508,7 @@
             rhs = jnp.concatenate(parts, axis=1)
             send_solved(0, 0, dot_nt(rhs, pinv[:, :(d + 1) * (panel_rows // pieces)]))
         if panels > 1:
-            departed_so((panels - 1) * owners)
+            departed_rest((panels - 1) * owners)
         w_departed(d, 0)
 
     for d in range(pieces):
@@ -536,7 +551,7 @@
                 @pl.when(k > position if fine else k != position)
                 def _():
                     fn(done + k)
-            each(owners, lambda k: below(owners - 1 - k, lambda c: rh_copy(c_me, c).start()))
+            each(owners, lambda k: below(k, lambda c: rh_copy(c_me, c).start()))
             if fine:
                 acc[...] = jnp.zeros_like(acc)
                 rhsrecv[position] = rhssend[...]
@@ -556,7 +571,7 @@
             if later:
                 for h in range(halves):
                     send_solved(panel, h, result[:, h * half_rows:(h + 1) * half_rows])
-                departed_so(later)
+                departed_rest(later)
             else:
                 sol_ref[...] = result
             each(owners, lambda k: below(k, lambda c: rh_copy(c_me, c).wait_send()))
@@ -643,7 +658,7 @@
         pltpu.VMEM((tcols, own_rows), F32),
         dma((10,)), dma((n_cen // chunk,)),
         dma((2,)), dma((2,)), dma((2,)), dma((2,)), dma((2,)), dma((1 + n_ctr,)), dma((2,)),
-        dma((1,)), dma((owners * (panels - 1) * halves,)),
+        dma((2,)), dma((owners * (panels - 1) * halves,)),
         dma((owners,)), dma((owners,)),
     ]
     grad, solved = pl.pallas_call(

time: 34.4 us -> 34.1 us (level)
  no operation moved by 1% of the time
where the time goes in v6:
time: 34.1 us; the launch traced here: 33.9 us
  Pallas kernels  33.2 us (97%)
  between operations  0.64 us (2%)
    pallas_call x1, Pallas kernels, body(): pl.pallas_call(functools.partial(kernel, n_pts, n_ctr, panels, chunk, 512...  32.4 us
    pallas_call x1, Pallas kernels, body(): pl.pallas_call(emit, out_shape=(jax.ShapeDtypeStruct((tcols, n_cen), F32)...  0.82 us

profile of v6, /device:TPU:26, one launch (start us, length us, event | category | flops | bytes accessed | tf_op | source)
XLA Modules:
  0.0 33.9 jit_solution(7357976480713142610)
XLA Ops:
  0.6 32.4 %falkon.1 = (f32[32,4096]{1,0:T(8,128)S(1)}, f32[32,512]{1,0:T(8,128)S(1)}) custom-call(bf16[16,512]{1,0:T(8,128)(2,1)} %pts_hbm.1, s32[1,16]{1,0:T(1,128)} %bitcast.8, f32[16,128]{1,0:T(8,128)} %tgt_hbm.1, f32[1,8]{1,0:T(1,128)} %bitcast.9, f32[1,512]{1,0:T(1,128)} %bitcast.7, s32[32,128]{1,0:T(8,128)} %bitcast.6, bf16[4096,512]{1,0:T(8,128)(2,1)} %cen_hbm.1, ...), custom_call_target="tpu_custom_call" | custom-call | tf_op jit(solution)/shard_map/falkon/pallas_call | solution.py:664
  33.0 0.8 %emit.1 = (f32[32,4096]{1,0:T(8,128)}, f32[32,512]{1,0:T(8,128)}) custom-call(f32[32,4096]{1,0:T(8,128)S(1)} %get-tuple-element.6.grad_ref, f32[32,512]{1,0:T(8,128)S(1)} %get-tuple-element.7.sol_ref), custom_call_target="tpu_custom_call" | custom-call | tf_op jit(solution)/shard_map/emit/pallas_call | solution.py:681

commit v7 on v6

--- a/solution.py
+++ b/solution.py
@@ -536,11 +536,13 @@
                     wblk[g] = turned[g * tcols:(g + 1) * tcols]
                 own = wblk[offset // part_len]
             if fine:
-                for b in range(done):
+                turn = jnp.where(c_me == n_ctr - 1, owners // 2, 0)
+                for step in range(done):
+                    b = lax.rem(step + turn, done)
                     for h in range(halves):
                         so_copy(b, b, h).wait_recv()
-                        begin = b * own_rows + h * half_rows
-                        own = own - dot_nt(solrecv[b * halves + h], fac[:, begin:begin + half_rows])
+                        begin = pl.multiple_of(b * own_rows + h * half_rows, half_rows)
+                        own = own - dot_nt(solrecv[b * halves + h], fac[:, pl.ds(begin, half_rows)])
             else:
                 each(done, lambda k: so_copy(k, k, 0).wait_recv())
                 solved = jnp.concatenate([solrecv[b] for b in range(done)], axis=1)

time: 34.1 us -> 34.1 us (level)
  no operation moved by 1% of the time
where the time goes in v7:
time: 34.1 us; the launch traced here: 33.9 us
  Pallas kernels  33.2 us (97%)
  between operations  0.64 us (2%)
    pallas_call x1, Pallas kernels, body(): pl.pallas_call(functools.partial(kernel, n_pts, n_ctr, panels, chunk, 512...  32.4 us
    pallas_call x1, Pallas kernels, body(): pl.pallas_call(emit, out_shape=(jax.ShapeDtypeStruct((tcols, n_cen), F32)...  0.82 us

profile of v7, /device:TPU:26, one launch (start us, length us, event | category | flops | bytes accessed | tf_op | source)
XLA Modules:
  0.0 33.9 jit_solution(10570079963892874673)
XLA Ops:
  0.6 32.4 %falkon.1 = (f32[32,4096]{1,0:T(8,128)S(1)}, f32[32,512]{1,0:T(8,128)S(1)}) custom-call(bf16[16,512]{1,0:T(8,128)(2,1)} %pts_hbm.1, s32[1,16]{1,0:T(1,128)} %bitcast.8, f32[16,128]{1,0:T(8,128)} %tgt_hbm.1, f32[1,8]{1,0:T(1,128)} %bitcast.9, f32[1,512]{1,0:T(1,128)} %bitcast.7, s32[32,128]{1,0:T(8,128)} %bitcast.6, bf16[4096,512]{1,0:T(8,128)(2,1)} %cen_hbm.1, ...), custom_call_target="tpu_custom_call" | custom-call | tf_op jit(solution)/shard_map/falkon/pallas_call | solution.py:666
  33.0 0.8 %emit.1 = (f32[32,4096]{1,0:T(8,128)}, f32[32,512]{1,0:T(8,128)}) custom-call(f32[32,4096]{1,0:T(8,128)S(1)} %get-tuple-element.6.grad_ref, f32[32,512]{1,0:T(8,128)S(1)} %get-tuple-element.7.sol_ref), custom_call_target="tpu_custom_call" | custom-call | tf_op jit(solution)/shard_map/emit/pallas_call | solution.py:683
